TPU v7x, 256 devices: a whole 4x4x8 slice. The times are simulated.
256 devices in a mesh: dp: 16 (over y, x_lo, core), cells: 16 (over z, x_hi).
Axes of the slice: x: 4 (x_hi: 2, x_lo: 2; x = x_hi * 2 + x_lo), y: 4, z: 8, core: 2. Of those that a mesh axis runs over, the one named last changes fastest.
Arguments:
- source_field: bfloat16 [48, 8, 12288], P(None, None, 'cells'), may hold values from -85 to 85, as said below
- receiver_field: bfloat16 [512, 8, 12288], P('dp', None, 'cells'), may hold values from -6 to 6
- source_index: int32 [8192], P('dp'), may hold values from 0 to 47
- receiver_index: int32 [8192], P('dp'), may hold values from 0 to 511, as said below
- observed: float32 [8192], P('dp'), may hold values from -6 to 6
- noise_code: int32 [8, 8192], P(None, 'dp'), may hold values from -4096 to 4096
- huber_code: int32 [8], replicated, may hold values from 8 to 40
- start_model: float32 [12288], P('cells'), may hold values from -6 to 6
Outputs:
- models: float32 [8, 12288], P(None, 'cells')
Inputs may be any that keep to these rules, and one draw needn't show every extreme that they name: `source_field`: entries of order one to ten; the scale varies from cell to cell. `receiver_index`: in each aligned block of 512 data, exactly 512 // 16 data name a receiver in each range [j * 32, (j + 1) * 32).
All inputs are finite; a program needn't handle non-finite values.
Results may differ from a plain program's by a relative error of at most 0.0011.
Values may be sent and summed in bfloat16 or wider, within the bound.
A program may use at most 64 MiB of HBM per device.

v0:
```python
import math

import jax
import jax.numpy as jnp
from jax import lax
from jax.sharding import PartitionSpec as P

ITERS = 2


def on_device(
    source_field,
    receiver_field,
    source_index,
    receiver_index,
    observed,
    noise_code,
    huber_code,
    start_model,
):
    count = huber_code.shape[0]
    thresh = (huber_code.astype(jnp.float32) / 16.0)[:, None]
    shifted = observed[None, :] + noise_code.astype(jnp.float32) / 4096.0
    receivers = lax.all_gather(receiver_field, "dp", axis=0, tiled=True)
    cells_local = source_field.shape[2]
    cells_total = cells_local * lax.axis_size("cells")
    components = source_field.shape[1]
    total = jnp.zeros((source_index.shape[0], cells_local), jnp.float32)
    for component in range(components):
        factor = 1.0 if component % 2 == 0 else -1.0
        source_part = source_field[source_index, component, :].astype(jnp.float32)
        receiver_part = receivers[receiver_index, component, :].astype(jnp.float32)
        total = total + factor * (source_part * receiver_part)
    kernel = (total * (0.2 / math.sqrt(components * cells_total))).astype(jnp.bfloat16)
    models = jnp.broadcast_to(start_model[None, :], (count, cells_local))
    velocity = jnp.zeros((count, cells_local), jnp.float32)
    for iteration in range(ITERS):
        model_half = models.astype(jnp.bfloat16)
        partial_sum = lax.dot_general(
            model_half, kernel, (((1,), (1,)), ((), ())), preferred_element_type=jnp.float32
        )
        predicted = lax.psum(partial_sum, "cells")
        weighted = jnp.clip(predicted - shifted, -thresh, thresh).astype(jnp.bfloat16)
        gradient_part = jnp.dot(weighted, kernel, preferred_element_type=jnp.float32)
        gradient = lax.psum(gradient_part, "dp")
        squares = lax.psum(jnp.sum(gradient * gradient, axis=1), "cells")
        scale_now = jnp.sqrt(squares / cells_total + 1e-06)[:, None]
        velocity = 0.9 * velocity + gradient / scale_now
        models = models - 0.1 * velocity
    return models


def solution(mesh):
    placed = (
        P(None, None, "cells"),
        P("dp", None, "cells"),
        P("dp"),
        P("dp"),
        P("dp"),
        P(None, "dp"),
        P(),
        P("cells"),
    )
    return jax.shard_map(
        on_device, mesh=mesh, in_specs=placed, out_specs=P(None, "cells"), check_vma=False
    )
```

profile of v0, /device:TPU:4, one launch (start us, length us, event | category | flops | bytes accessed | tf_op | source)
XLA Modules:
  0.0 488.1 jit_solution(16038923808687295108)
XLA Ops:
  6.5 0.7 all-gather.2.cloned.1.call-update
  7.3 0.7 fusion.17
  8.0 4.6 gather_fusion
  12.5 4.6 gather_fusion.10
  17.1 7.2 %gather_fusion.12 = bf16[512,768]{1,0:T(8,128)(2,1)} fusion(bf16[48,8,768]{2,1,0:T(8,128)(2,1)S(1)} %copy-done, s32[512]{0:T(512)S(1)} %get-tuple-element.12), kind=kCustom, calls=%fused_computation.12 | custom fusion | bytes 1576960 | tf_op jit(solution)/shard_map/gather | solution.py:31
  24.3 7.1 %gather_fusion.14 = bf16[512,768]{1,0:T(8,128)(2,1)} fusion(bf16[48,8,768]{2,1,0:T(8,128)(2,1)S(1)} %copy-done, s32[512]{0:T(512)S(1)} %get-tuple-element.6), kind=kCustom, calls=%fused_computation.14 | custom fusion | bytes 1576960 | tf_op jit(solution)/shard_map/gather | solution.py:31
  31.4 7.1 %gather_fusion.2 = bf16[512,768]{1,0:T(8,128)(2,1)} fusion(bf16[48,8,768]{2,1,0:T(8,128)(2,1)S(1)} %copy-done, s32[512]{0:T(512)S(1)} %get-tuple-element.7), kind=kCustom, calls=%fused_computation.2 | custom fusion | bytes 1576960 | tf_op jit(solution)/shard_map/gather | solution.py:31
  38.5 7.1 %gather_fusion.4 = bf16[512,768]{1,0:T(8,128)(2,1)} fusion(bf16[48,8,768]{2,1,0:T(8,128)(2,1)S(1)} %copy-done, s32[512]{0:T(512)S(1)} %get-tuple-element.8), kind=kCustom, calls=%fused_computation.4 | custom fusion | bytes 1576960 | tf_op jit(solution)/shard_map/gather | solution.py:31
  45.6 7.2 %gather_fusion.6 = bf16[512,768]{1,0:T(8,128)(2,1)} fusion(bf16[48,8,768]{2,1,0:T(8,128)(2,1)S(1)} %copy-done, s32[512]{0:T(512)S(1)} %get-tuple-element.9), kind=kCustom, calls=%fused_computation.6 | custom fusion | bytes 1576960 | tf_op jit(solution)/shard_map/gather | solution.py:31
  52.8 7.1 %gather_fusion.8 = bf16[512,768]{1,0:T(8,128)(2,1)} fusion(bf16[48,8,768]{2,1,0:T(8,128)(2,1)S(1)} %copy-done, s32[512]{0:T(512)S(1)} %get-tuple-element.10), kind=kCustom, calls=%fused_computation.8 | custom fusion | bytes 1576960 | tf_op jit(solution)/shard_map/gather | solution.py:31
  60.0 9.8 %gather_fusion.1 = bf16[512,768]{1,0:T(8,128)(2,1)} fusion(bf16[512,8,768]{2,1,0:T(8,128)(2,1)} %all-gather.2.cloned.1.call-done, s32[512]{0:T(512)S(1)} %get-tuple-element.13), kind=kCustom, calls=%fused_computation.1 | custom fusion | bytes 1576960 | tf_op jit(solution)/shard_map/gather | solution.py:32
  69.8 9.8 %gather_fusion.11 = bf16[512,768]{1,0:T(8,128)(2,1)} fusion(bf16[512,8,768]{2,1,0:T(8,128)(2,1)} %all-gather.2.cloned.1.call-done, s32[512]{0:T(512)S(1)} %get-tuple-element.19), kind=kCustom, calls=%fused_computation.11 | custom fusion | bytes 1576960 | tf_op jit(solution)/shard_map/gather | solution.py:32
  79.6 9.8 %gather_fusion.13 = bf16[512,768]{1,0:T(8,128)(2,1)} fusion(bf16[512,8,768]{2,1,0:T(8,128)(2,1)} %all-gather.2.cloned.1.call-done, s32[512]{0:T(512)S(1)} %get-tuple-element.20), kind=kCustom, calls=%fused_computation.13 | custom fusion | bytes 1576960 | tf_op jit(solution)/shard_map/gather | solution.py:32
  89.3 9.8 %gather_fusion.15 = bf16[512,768]{1,0:T(8,128)(2,1)} fusion(bf16[512,8,768]{2,1,0:T(8,128)(2,1)} %all-gather.2.cloned.1.call-done, s32[512]{0:T(512)S(1)} %get-tuple-element.14), kind=kCustom, calls=%fused_computation.15 | custom fusion | bytes 1576960 | tf_op jit(solution)/shard_map/gather | solution.py:32
  99.1 9.8 %gather_fusion.3 = bf16[512,768]{1,0:T(8,128)(2,1)} fusion(bf16[512,8,768]{2,1,0:T(8,128)(2,1)} %all-gather.2.cloned.1.call-done, s32[512]{0:T(512)S(1)} %get-tuple-element.15), kind=kCustom, calls=%fused_computation.3 | custom fusion | bytes 1576960 | tf_op jit(solution)/shard_map/gather | solution.py:32
  108.9 9.8 %gather_fusion.5 = bf16[512,768]{1,0:T(8,128)(2,1)} fusion(bf16[512,8,768]{2,1,0:T(8,128)(2,1)} %all-gather.2.cloned.1.call-done, s32[512]{0:T(512)S(1)} %get-tuple-element.16), kind=kCustom, calls=%fused_computation.5 | custom fusion | bytes 1576960 | tf_op jit(solution)/shard_map/gather | solution.py:32
  118.7 9.7 %gather_fusion.7 = bf16[512,768]{1,0:T(8,128)(2,1)} fusion(bf16[512,8,768]{2,1,0:T(8,128)(2,1)} %all-gather.2.cloned.1.call-done, s32[512]{0:T(512)S(1)} %get-tuple-element.17), kind=kCustom, calls=%fused_computation.7 | custom fusion | bytes 1576960 | tf_op jit(solution)/shard_map/gather | solution.py:32
  128.4 9.8 %gather_fusion.9 = bf16[512,768]{1,0:T(8,128)(2,1)} fusion(bf16[512,8,768]{2,1,0:T(8,128)(2,1)} %all-gather.2.cloned.1.call-done, s32[512]{0:T(512)S(1)} %get-tuple-element.18), kind=kCustom, calls=%fused_computation.9 | custom fusion | bytes 1576960 | tf_op jit(solution)/shard_map/gather | solution.py:32
  138.2 6.0 %multiply_convert_fusion = bf16[512,768]{1,0:T(8,128)(2,1)S(1)} fusion(bf16[512,768]{1,0:T(8,128)(2,1)} %gather_fusion.15, bf16[512,768]{1,0:T(8,128)(2,1)} %gather_fusion.14, bf16[512,768]{1,0:T(8,128)(2,1)} %gather_fusion.13, bf16[512,768]{1,0:T(8,128)(2,1)} %gather_fusion.12, bf16[512,768]{1,0:T(8,128)(2,1)} %gather_fusion.11, ...), kind=kLoop, calls=%fused_computation.16 | loop fusion | flops 14548992 | bytes 13369344 | tf_op jit(solution)/shard_map/convert_element_type | solution.py:34
  144.2 0.3 convolution_bitcast_fusion
  144.5 74.7 %psum.42 = f32[8,512]{1,0:T(8,128)S(1)} all-reduce(f32[8,512]{1,0:T(8,128)S(1)} %convolution_bitcast_fusion), channel_id=1, replica_groups=mesh['dp'=16,'cells'=16] {'cells'}, use_global_device_ids=true, to_apply=%region_0.0 | all-reduce | flops 4096 | bytes 32768 | tf_op jit(solution)/shard_map/psum | solution.py:42
  219.2 0.2 fusion.5
  219.5 52.9 %psum.43 = f32[8,768]{1,0:T(8,128)S(1)} all-reduce(f32[8,768]{1,0:T(8,128)S(1)} %fusion.5), channel_id=1, replica_groups=mesh['dp'=16,'cells'=16] {'dp'}, use_global_device_ids=true, to_apply=%region_1.2 | all-reduce | flops 6144 | bytes 49152 | tf_op jit(solution)/shard_map/psum | solution.py:45
  272.4 0.1 multiply_reduce_fusion.1
  272.5 42.5 %psum.44 = f32[8]{0:T(128)S(1)} all-reduce(f32[8]{0:T(128)S(1)} %multiply_reduce_fusion.1), channel_id=1, replica_groups=mesh['dp'=16,'cells'=16] {'cells'}, use_global_device_ids=true, to_apply=%region_3.4 | all-reduce | flops 8 | bytes 64 | tf_op jit(solution)/shard_map/psum | solution.py:46
  315.0 0.3 fusion.1
  315.3 69.7 %psum.45 = f32[8,512]{1,0:T(8,128)S(1)} all-reduce(f32[8,512]{1,0:T(8,128)S(1)} %fusion.1), channel_id=1, replica_groups=mesh['dp'=16,'cells'=16] {'cells'}, use_global_device_ids=true, to_apply=%region_4.5 | all-reduce | flops 4096 | bytes 32768 | tf_op jit(solution)/shard_map/psum | solution.py:42
  385.0 0.2 fusion.6
  385.3 52.9 %psum.46 = f32[8,768]{1,0:T(8,128)S(1)} all-reduce(f32[8,768]{1,0:T(8,128)S(1)} %fusion.6), channel_id=1, replica_groups=mesh['dp'=16,'cells'=16] {'dp'}, use_global_device_ids=true, to_apply=%region_5.6 | all-reduce | flops 6144 | bytes 49152 | tf_op jit(solution)/shard_map/psum | solution.py:45
  438.2 0.1 multiply_reduce_fusion
  438.3 42.2 %psum.47 = f32[8]{0:T(128)S(1)} all-reduce(f32[8]{0:T(128)S(1)} %multiply_reduce_fusion), channel_id=1, replica_groups=mesh['dp'=16,'cells'=16] {'cells'}, use_global_device_ids=true, to_apply=%region_7.8 | all-reduce | flops 8 | bytes 64 | tf_op jit(solution)/shard_map/psum | solution.py:46
  480.5 0.7 multiply_subtract_fusion
  (19 shorter events, 0.1 us)
Async XLA Ops:
  6.5 1.4 copy-start
  6.5 53.4 %all-gather.2.cloned.1.call-start = ((), (), s32[]{:S(2)}) async-start(), calls=%async_computation | async-start | bytes 6684672 | tf_op jit(solution)/shard_map/all_gather | solution.py:24
  52.8 7.1 %copy-start.2 = (f32[768]{0:T(1024)S(1)}, f32[768]{0:T(1024)}, u32[]{:S(2)}) copy-start(f32[768]{0:T(1024)} %param.15) | copy-start | bytes 9220
  52.8 7.1 %copy-start.5 = (s32[8]{0:T(128)S(1)}, s32[8]{0:T(128)}, u32[]{:S(2)}) copy-start(s32[8]{0:T(128)} %param.14) | copy-start | bytes 100
  52.8 7.2 %copy-start.4 = (s32[512]{0:T(512)S(1)}, s32[512]{0:T(512)}, u32[]{:S(2)}) copy-start(s32[512]{0:T(512)} %param.11) | copy-start | bytes 6148
  138.2 81.0 %copy-start.1 = (s32[8,512]{1,0:T(8,128)S(1)}, s32[8,512]{1,0:T(8,128)}, u32[]{:S(2)}) copy-start(s32[8,512]{1,0:T(8,128)} %param.13) | copy-start | bytes 49156
  138.2 81.0 %copy-start.3 = (f32[512]{0:T(512)S(1)}, f32[512]{0:T(512)}, u32[]{:S(2)}) copy-start(f32[512]{0:T(512)} %param.12) | copy-start | bytes 6148
Sparse Core Ops, SparseCore 0:
  9.2 47.6 all-gather.1
where the time goes:
time: 489 us; the launch traced here: 488 us
  blocking collectives  335 us (69%)
  local copies, waits for them, and re-layouts  130 us (27%)
  between operations  13.5 us (3%)
  other arithmetic  7.68 us (2%)
    psum x2, blocking collectives, on_device(): predicted = lax.psum(partial_sum, 'cells')  144 us
    psum x2, blocking collectives, on_device(): gradient = lax.psum(gradient_part, 'dp')  106 us
    psum x2, blocking collectives, on_device(): squares = lax.psum(jnp.sum(gradient * gradient, axis=1), 'cells')  84.7 us
    gather x8, local copies, waits for them, and re-layouts, on_device(): receiver_part = receivers[receiver_index, component, :].astype(jnp.float32)  78.2 us
    gather x8, local copies, waits for them, and re-layouts, on_device(): source_part = source_field[source_index, component, :].astype(jnp.float32)  51.9 us
  transfers between devices with their start and end apart: 1, of which 0 were waited for; matrix products, arithmetic and copies ran while one was open for 11% of the time, Pallas kernels for 0%

commit v1 on v0

v1 whole, which is shorter than its diff:
```python
import functools
import math

import jax
import jax.numpy as jnp
from jax import lax
from jax.experimental import pallas as pl
from jax.experimental.pallas import tpu as pltpu
from jax.sharding import PartitionSpec as P

F32 = jnp.float32
BF16 = jnp.bfloat16
GROUP = 16
COMP = 8
REAL = 8
MESH = pl.DeviceIdType.MESH


def iota(shape, axis):
    return lax.broadcasted_iota(jnp.int32, shape, axis)


def dot(a, b):
    return jnp.dot(a, b, preferred_element_type=F32)


def dot_nt(a, b):
    return lax.dot_general(a, b, (((1,), (1,)), ((), ())), preferred_element_type=F32)


def split_halves(table):
    high = table.astype(BF16).astype(F32)
    return jnp.where(iota(table.shape, 1) < 64, high, table - high).astype(BF16)


def body(
    cells_total,
    src_ref,
    rec_ref,
    sidx_ref,
    ridx_ref,
    obs_ref,
    noise_ref,
    huber_ref,
    start_ref,
    out_ref,
    sc,
    rc,
    data_s,
    data_r,
    tab_s,
    tab_r,
    g1_s,
    g1_r,
    g1_a,
    dl_s,
    dl_r,
    q1_s,
    q1_r,
    g2_s,
    g2_r,
    g2_a,
    q2_s,
    q2_r,
    send_sem,
    recv_sem,
):
    me_dp = lax.axis_index("dp")
    me_cells = lax.axis_index("cells")
    cells = start_ref.shape[1]
    n_data = sidx_ref.shape[1]
    scale = 0.2 / math.sqrt(COMP * cells_total)

    def peer(axis, offset):
        me = me_dp if axis == "dp" else me_cells
        return lax.rem(me + offset, GROUP)

    barrier = pltpu.get_barrier_semaphore()

    def greet(offset, carry):
        for axis in ("dp", "cells"):
            pl.semaphore_signal(
                barrier, inc=1, device_id={axis: peer(axis, offset)}, device_id_type=MESH
            )
        return carry

    lax.fori_loop(1, GROUP, greet, 0)

    def send_all(axis, phase, src_of, dst_of):
        def one(offset, carry):
            other = peer(axis, offset)
            pltpu.make_async_remote_copy(
                src_ref=src_of(other),
                dst_ref=dst_of(offset),
                send_sem=send_sem.at[phase],
                recv_sem=recv_sem.at[phase],
                device_id={axis: other},
                device_id_type=MESH,
            ).start()
            return carry

        lax.fori_loop(1, GROUP, one, 0)

    def wait_all(sem, phase, ref):
        part = ref.at[pl.ds(0, GROUP - 1)]
        pltpu.make_async_copy(part, part, sem.at[phase]).wait()

    pick = (
        (iota((128, 128), 0) % 16) * COMP + iota((128, 128), 0) // 16 == iota((128, 128), 1)
    ).astype(F32).astype(BF16)
    zero_rows = jnp.zeros((16, cells), BF16)
    for chunk in range(3):
        rows = dot(pick, src_ref[128 * chunk : 128 * chunk + 128, :]).astype(BF16)
        for c in range(COMP):
            part = rows[16 * c : 16 * c + 16, :]
            sc[c, 16 * chunk : 16 * chunk + 16, :] = part
            sc[c, 64 + 16 * chunk : 80 + 16 * chunk, :] = part
    for c in range(COMP):
        sc[c, 48:64, :] = zero_rows
        sc[c, 112:128, :] = zero_rows
    for chunk in range(2):
        rows = dot(pick, rec_ref[128 * chunk : 128 * chunk + 128, :])
        for c in range(COMP):
            part = rows[16 * c : 16 * c + 16, :]
            rc[c, 16 * chunk : 16 * chunk + 16, :] = part if c % 2 == 0 else -part

    start = start_ref[...]
    start_half = start.astype(BF16).astype(F32)
    table = jnp.zeros((64, 128), F32)
    for c in range(COMP):
        exact = rc[c] * start_half
        high = exact.astype(BF16)
        low = (exact - high.astype(F32)).astype(BF16)
        table = table + dot_nt(jnp.concatenate([high, low], axis=0), sc[c])
    table = (table[0:32] + table[32:64]) * scale
    left = iota((8, 128), 1) < 64
    tab_s[0] = jnp.where(left, table[0:8], table[8:16])
    tab_s[1] = jnp.where(left, table[16:24], table[24:32])

    pl.semaphore_wait(barrier, 2 * (GROUP - 1))
    send_all("cells", 1, lambda o: tab_s, lambda off: tab_r.at[off - 1])

    owner = ridx_ref[...] // 32
    local = ridx_ref[...] % 32
    member = (iota((16, n_data), 0) == owner).astype(F32)
    before = (iota((n_data, n_data), 0) < iota((n_data, n_data), 1)).astype(F32).astype(BF16)
    rank = jnp.sum(member * dot(member.astype(BF16), before), axis=0, keepdims=True)
    place = (128 * (owner // 4) + 32 * ((owner + me_dp) % 4)).astype(F32) + rank
    move = (iota((n_data, n_data), 0).astype(F32) == place).astype(F32).astype(BF16)
    shifted = obs_ref[...] + noise_ref[...].astype(F32) / 4096.0
    high = shifted.astype(BF16).astype(F32)
    middle = (shifted - high).astype(BF16).astype(F32)
    low = shifted - high - middle
    row8 = iota((8, n_data), 0)
    index_rows = jnp.where(
        row8 == 0,
        sidx_ref[...].astype(F32),
        jnp.where(row8 == 1, local.astype(F32), 0.0),
    )
    moved = dot_nt(jnp.concatenate([high, middle, low, index_rows], axis=0).astype(BF16), move)
    shifted = moved[0:8] + moved[8:16] + moved[16:24]
    for t in range(4):
        data_s[t, 0:8, :] = shifted[:, 128 * t : 128 * t + 128]
        data_s[t, 8:16, :] = moved[24:32, 128 * t : 128 * t + 128]
    send_all("dp", 0, lambda o: data_s.at[o // 4], lambda off: data_r.at[off - 1])
    data_r[GROUP - 1] = data_s[me_dp // 4]
    wait_all(recv_sem, 0, data_r)
    quarter = iota((16, 128), 1) // 32
    tiles = []
    for t in range(4):
        tile = data_r[4 * t]
        for o in range(4 * t + 2, 4 * t + 5):
            here = lax.rem(2 * me_dp + 32 - o, 4)
            tile = jnp.where(quarter == here, data_r[o - 1], tile)
        tiles.append(tile)
    data = jnp.concatenate(tiles, axis=1)
    shifted = data[0:8]
    source = data[8:9].astype(jnp.int32)
    receiver = data[9:10].astype(jnp.int32)
    is_source = (iota((128, n_data), 0) % 64 == source).astype(F32).astype(BF16)
    is_receiver = (iota((32, n_data), 0) == receiver).astype(F32)
    limit = jnp.zeros((REAL, n_data), F32)
    for k in range(REAL):
        limit = jnp.where(row8 == k, huber_ref[k].astype(F32) / 16.0, limit)

    wait_all(recv_sem, 1, tab_r)
    packed = tab_s[...]
    for o in range(GROUP - 1):
        packed = packed + tab_r[o]
    rows = []
    for t in range(2):
        here = packed[t]
        turned = pltpu.roll(here, 64, 1)
        rows.append(jnp.where(left, here, turned))
        rows.append(jnp.where(left, turned, here))
    spread = dot(split_halves(jnp.concatenate(rows, axis=0)), is_source)
    predicted = jnp.sum(spread * is_receiver, axis=0, keepdims=True)

    def gradient(predicted, out):
        weighted = jnp.clip(predicted - shifted, -limit, limit).astype(BF16).astype(F32)
        spread = [(weighted[k : k + 1, :] * is_receiver).astype(BF16) for k in range(REAL)]
        pairs = split_halves(dot_nt(jnp.concatenate(spread, axis=0), is_source))
        for b in range(cells // 256):
            lanes = slice(256 * b, 256 * b + 256)
            total = [jnp.zeros((8, 256), F32) for k in range(REAL)]
            for c in range(COMP):
                mixed = dot(pairs, sc[c, :, lanes])
                field = rc[c, :, lanes]
                for k in range(REAL):
                    product = mixed[32 * k : 32 * k + 32] * field
                    total[k] = total[k] + (
                        (product[0:8] + product[8:16]) + (product[16:24] + product[24:32])
                    )
            for k in range(REAL):
                row = jnp.sum(total[k], axis=0, keepdims=True) * scale
                for half in range(2):
                    t = 2 * b + half
                    at = 128 * (t % 3)
                    out[2 * k + t // 3, :, at : at + 128] = row[:, 128 * half : 128 * half + 128]

    def reduce_gradient(phase, part, arrived, whole):
        send_all("dp", phase, lambda o: part.at[o], lambda off: arrived.at[off - 1])
        mine = part[me_dp]
        wait_all(recv_sem, phase, arrived)
        for o in range(GROUP - 1):
            mine = mine + arrived[o]
        whole[me_dp] = mine
        send_all("dp", phase + 1, lambda o: whole.at[me_dp], lambda off: whole.at[me_dp])
        wait_all(recv_sem, phase + 1, whole)
        return [
            jnp.concatenate([whole[2 * k], whole[2 * k + 1]], axis=1) for k in range(REAL)
        ]

    def square_sums(rows):
        total = jnp.zeros((1, 128), F32)
        for k in range(REAL):
            one = jnp.sum(rows[k] * rows[k], axis=1, keepdims=True)
            total = jnp.where(iota((1, 128), 1) == k, one, total)
        return total

    def inverse_scale(own, arrived):
        total = own
        for o in range(GROUP - 1):
            total = total + arrived[o]
        diagonal = iota((8, 128), 0) == iota((8, 128), 1)
        column = jnp.sum(jnp.where(diagonal, total, 0.0), axis=1, keepdims=True)
        return 1.0 / jnp.sqrt(column / cells_total + 1e-06)

    gradient(predicted, g1_s)
    first = reduce_gradient(2, g1_s, g1_r, g1_a)

    table = jnp.zeros((32 * REAL, 128), F32)
    for c in range(COMP):
        field = rc[c]
        scaled = [(field * first[k]).astype(BF16) for k in range(REAL)]
        table = table + dot_nt(jnp.concatenate(scaled, axis=0), sc[c])
    spread = dot(split_halves(table * scale), is_source)
    change = jnp.concatenate(
        [
            jnp.sum(spread[32 * k : 32 * k + 32] * is_receiver, axis=0, keepdims=True)
            for k in range(REAL)
        ],
        axis=0,
    )
    half = n_data // 2
    dl_s[...] = jnp.concatenate([change[:, :half], change[:, half:]], axis=0).astype(BF16)
    q1_s[...] = square_sums(first)
    send_all("cells", 4, lambda o: dl_s, lambda off: dl_r.at[off - 1])
    send_all("cells", 5, lambda o: q1_s, lambda off: q1_r.at[off - 1])
    wait_all(recv_sem, 5, q1_r)
    inverse1 = inverse_scale(q1_s[...], q1_r)
    wait_all(recv_sem, 4, dl_r)
    total = dl_s[...].astype(F32)
    for o in range(GROUP - 1):
        total = total + dl_r[o].astype(F32)
    change = jnp.concatenate([total[0:8], total[8:16]], axis=1)
    gradient(predicted - 0.1 * (change * inverse1), g2_s)
    second = reduce_gradient(6, g2_s, g2_r, g2_a)
    q2_s[...] = square_sums(second)
    send_all("cells", 8, lambda o: q2_s, lambda off: q2_r.at[off - 1])
    velocity = jnp.concatenate(first, axis=0) * inverse1
    base = (start - 0.1 * velocity) - 0.1 * (0.9 * velocity)
    step = jnp.concatenate(second, axis=0)
    wait_all(recv_sem, 8, q2_r)
    out_ref[...] = base - 0.1 * (step * inverse_scale(q2_s[...], q2_r))

    for phase, ref in enumerate((data_r, tab_r, g1_r, g1_a, dl_r, q1_r, g2_r, g2_a, q2_r)):
        wait_all(send_sem, phase, ref)


def on_device(source, receiver, source_index, receiver_index, observed, noise, huber, start):
    cells = start.shape[0]
    n_data = source_index.shape[0]
    near = GROUP - 1
    vmem = pl.BlockSpec(memory_space=pltpu.VMEM)
    row = pltpu.VMEM((1, 128), F32)
    rows = pltpu.VMEM((near, 1, 128), F32)
    chunk = REAL * cells // GROUP
    return pl.pallas_call(
        functools.partial(body, cells * GROUP),
        out_shape=jax.ShapeDtypeStruct((REAL, cells), F32),
        in_specs=[vmem] * 6 + [pl.BlockSpec(memory_space=pltpu.SMEM), vmem],
        out_specs=vmem,
        scratch_shapes=[
            pltpu.VMEM((COMP, 128, cells), BF16),
            pltpu.VMEM((COMP, 32, cells), F32),
            pltpu.VMEM((4, 16, 128), F32),
            pltpu.VMEM((GROUP, 16, 128), F32),
            pltpu.VMEM((2, 8, 128), F32),
            pltpu.VMEM((near, 2, 8, 128), F32),
            pltpu.VMEM((GROUP, 1, chunk), F32),
            pltpu.VMEM((near, 1, chunk), F32),
            pltpu.VMEM((GROUP, 1, chunk), F32),
            pltpu.VMEM((16, n_data // 2), BF16),
            pltpu.VMEM((near, 16, n_data // 2), BF16),
            row,
            rows,
            pltpu.VMEM((GROUP, 1, chunk), F32),
            pltpu.VMEM((near, 1, chunk), F32),
            pltpu.VMEM((GROUP, 1, chunk), F32),
            row,
            rows,
            pltpu.SemaphoreType.DMA((9,)),
            pltpu.SemaphoreType.DMA((9,)),
        ],
        compiler_params=pltpu.CompilerParams(collective_id=0, has_side_effects=True),
    )(
        source.reshape(-1, cells),
        receiver.reshape(-1, cells),
        source_index.reshape(1, n_data),
        receiver_index.reshape(1, n_data),
        observed.reshape(1, n_data),
        noise,
        huber,
        start.reshape(1, cells),
    )


def solution(mesh):
    placed = (
        P(None, None, "cells"),
        P("dp", None, "cells"),
        P("dp"),
        P("dp"),
        P("dp"),
        P(None, "dp"),
        P(),
        P("cells"),
    )
    return jax.shard_map(
        on_device, mesh=mesh, in_specs=placed, out_specs=P(None, "cells"), check_vma=False
    )
```

time: 489 us -> 56.5 us (0.12)
  the two profiles are of different devices: /device:TPU:4 before, /device:TPU:1 now
where the time goes in v1:
time: 56.5 us; the launch traced here: 56.3 us
  Pallas kernels  53.7 us (95%)
  local copies, waits for them, and re-layouts  2.61 us (5%)
    pallas_call x1, Pallas kernels, on_device(): pl.pallas_call(functools.partial(body, cells * GROUP), out_shape=jax.Shap...  53.7 us
    unnamed x3, local copies, waits for them, and re-layouts  2.03 us

profile of v1, /device:TPU:1, one launch (start us, length us, event | category | flops | bytes accessed | tf_op | source)
XLA Modules:
  0.0 56.3 jit_solution(4027771792766225074)
XLA Ops:
  0.0 0.0 copy-start
  0.0 0.7 %copy-done = f32[768]{0:T(1024)S(1)} copy-done((f32[768]{0:T(1024)S(1)}, f32[768]{0:T(1024)}, u32[]{:S(2)}) %copy-start) | copy-done | bytes 3096
  0.7 0.6 %reshape.23.start_ref = f32[1,768]{1,0:T(1,128)} reshape(f32[768]{0:T(1024)S(1)} %copy-done) | data formatting | bytes 6144 | tf_op jit(solution)/shard_map/reshape | solution.py:335
  1.3 53.7 %shard_map.82 = f32[8,768]{1,0:T(8,128)} custom-call(bf16[384,768]{1,0:T(8,128)(2,1)} %bitcast.5, bf16[256,768]{1,0:T(8,128)(2,1)} %bitcast.6, s32[1,512]{1,0:T(1,128)} %bitcast.7, s32[1,512]{1,0:T(1,128)} %bitcast.8, f32[1,512]{1,0:T(1,128)} %bitcast.9, s32[8,512]{1,0:T(8,128)} %noise_ref.1, s32[8]{0:T(128)} %huber_ref.1, f32[1,768]{1,0:T(1,128)} %reshape.23.start_ref), custom_call_target="tpu_custom_call" | custom-call | tf_op jit(solution)/shard_map/pallas_call | solution.py:299
  55.0 1.3 %copy.10 = f32[8,768]{1,0:T(8,128)} copy(f32[8,768]{1,0:T(8,128)} %shard_map.82) | data formatting | bytes 49152
Async XLA Ops:
  0.0 0.7 %copy-start = (f32[768]{0:T(1024)S(1)}, f32[768]{0:T(1024)}, u32[]{:S(2)}) copy-start(f32[768]{0:T(1024)} %param.15) | copy-start | bytes 9220

commit v2 on v1

--- a/solution.py
+++ b/solution.py
@@ -14,6 +14,7 @@
 COMP = 8
 REAL = 8
 MESH = pl.DeviceIdType.MESH
+FAR_FIRST = sorted(range(1, GROUP), key=lambda o: -min(o, GROUP - o))
 
 
 def iota(shape, axis):
@@ -35,39 +36,15 @@
 
 def body(
     cells_total,
-    src_ref,
-    rec_ref,
-    sidx_ref,
-    ridx_ref,
-    obs_ref,
-    noise_ref,
-    huber_ref,
-    start_ref,
-    out_ref,
-    sc,
-    rc,
-    data_s,
-    data_r,
-    tab_s,
-    tab_r,
-    g1_s,
-    g1_r,
-    g1_a,
-    dl_s,
-    dl_r,
-    q1_s,
-    q1_r,
-    g2_s,
-    g2_r,
-    g2_a,
-    q2_s,
-    q2_r,
-    send_sem,
-    recv_sem,
+    *refs,
 ):
+    given, out_ref, held, refs = refs[:8], refs[8], refs[9:17], refs[17:]
+    src_ref, rec_ref, sidx_ref, ridx_ref, obs_ref, noise_ref, huber_ref, start_ref = held
+    sc, rc, grad, data_s, data_r, tab_s, tab_r, g1_s, g1_r, dl_s, dl_r, q1_s, q1_r = refs[:13]
+    g2_s, g2_r, q2_s, q2_r, send_sem, recv_sem, load_sem = refs[13:]
     me_dp = lax.axis_index("dp")
     me_cells = lax.axis_index("cells")
-    cells = start_ref.shape[1]
+    cells = src_ref.shape[1]
     n_data = sidx_ref.shape[1]
     scale = 0.2 / math.sqrt(COMP * cells_total)
 
@@ -77,17 +54,19 @@
 
     barrier = pltpu.get_barrier_semaphore()
 
-    def greet(offset, carry):
-        for axis in ("dp", "cells"):
+    for offset in FAR_FIRST:
+        for axis in ("cells", "dp"):
             pl.semaphore_signal(
                 barrier, inc=1, device_id={axis: peer(axis, offset)}, device_id_type=MESH
             )
-        return carry
-
-    lax.fori_loop(1, GROUP, greet, 0)
+    loads = [
+        pltpu.make_async_copy(a, b, load_sem.at[n]) for n, (a, b) in enumerate(zip(given, held))
+    ]
+    for n in (1, 7, 0, 2, 3, 4, 5, 6):
+        loads[n].start()
 
     def send_all(axis, phase, src_of, dst_of):
-        def one(offset, carry):
+        for offset in FAR_FIRST:
             other = peer(axis, offset)
             pltpu.make_async_remote_copy(
                 src_ref=src_of(other),
@@ -97,9 +76,6 @@
                 device_id={axis: other},
                 device_id_type=MESH,
             ).start()
-            return carry
-
-        lax.fori_loop(1, GROUP, one, 0)
 
     def wait_all(sem, phase, ref):
         part = ref.at[pl.ds(0, GROUP - 1)]
@@ -108,6 +84,13 @@
     pick = (
         (iota((128, 128), 0) % 16) * COMP + iota((128, 128), 0) // 16 == iota((128, 128), 1)
     ).astype(F32).astype(BF16)
+    loads[1].wait()
+    for chunk in range(2):
+        rows = dot(pick, rec_ref[128 * chunk : 128 * chunk + 128, :])
+        for c in range(COMP):
+            part = rows[16 * c : 16 * c + 16, :]
+            rc[c, 16 * chunk : 16 * chunk + 16, :] = part if c % 2 == 0 else -part
+    loads[0].wait()
     zero_rows = jnp.zeros((16, cells), BF16)
     for chunk in range(3):
         rows = dot(pick, src_ref[128 * chunk : 128 * chunk + 128, :]).astype(BF16)
@@ -118,13 +101,9 @@
     for c in range(COMP):
         sc[c, 48:64, :] = zero_rows
         sc[c, 112:128, :] = zero_rows
-    for chunk in range(2):
-        rows = dot(pick, rec_ref[128 * chunk : 128 * chunk + 128, :])
-        for c in range(COMP):
-            part = rows[16 * c : 16 * c + 16, :]
-            rc[c, 16 * chunk : 16 * chunk + 16, :] = part if c % 2 == 0 else -part
-
-    start = start_ref[...]
+
+    loads[7].wait()
+    start = jnp.concatenate([start_ref[n : n + 1, :] for n in range(cells // 128)], axis=1)
     start_half = start.astype(BF16).astype(F32)
     table = jnp.zeros((64, 128), F32)
     for c in range(COMP):
@@ -140,6 +119,8 @@
     pl.semaphore_wait(barrier, 2 * (GROUP - 1))
     send_all("cells", 1, lambda o: tab_s, lambda off: tab_r.at[off - 1])
 
+    for n in range(2, 7):
+        loads[n].wait()
     owner = ridx_ref[...] // 32
     local = ridx_ref[...] % 32
     member = (iota((16, n_data), 0) == owner).astype(F32)
@@ -196,6 +177,20 @@
     spread = dot(split_halves(jnp.concatenate(rows, axis=0)), is_source)
     predicted = jnp.sum(spread * is_receiver, axis=0, keepdims=True)
 
+    def fold(x):
+        half = x.shape[1] // 2
+        return jnp.concatenate([x[:, :half], x[:, half:]], axis=0)
+
+    def unfold(x):
+        half = x.shape[0] // 2
+        return jnp.concatenate([x[:half], x[half:]], axis=1)
+
+    def sum_slots(arrived):
+        parts = [arrived[o].astype(F32) for o in range(GROUP)]
+        while len(parts) > 1:
+            parts = [a + b for a, b in zip(parts[::2], parts[1::2])]
+        return parts[0]
+
     def gradient(predicted, out):
         weighted = jnp.clip(predicted - shifted, -limit, limit).astype(BF16).astype(F32)
         spread = [(weighted[k : k + 1, :] * is_receiver).astype(BF16) for k in range(REAL)]
@@ -212,47 +207,37 @@
                         (product[0:8] + product[8:16]) + (product[16:24] + product[24:32])
                     )
             for k in range(REAL):
-                row = jnp.sum(total[k], axis=0, keepdims=True) * scale
-                for half in range(2):
-                    t = 2 * b + half
-                    at = 128 * (t % 3)
-                    out[2 * k + t // 3, :, at : at + 128] = row[:, 128 * half : 128 * half + 128]
-
-    def reduce_gradient(phase, part, arrived, whole):
-        send_all("dp", phase, lambda o: part.at[o], lambda off: arrived.at[off - 1])
-        mine = part[me_dp]
+                grad[k : k + 1, lanes] = jnp.sum(total[k], axis=0, keepdims=True) * scale
+        whole = grad[...]
+        out[...] = fold(whole).astype(BF16)
+
+    def reduce_gradient(phase, part, arrived):
+        send_all("dp", phase, lambda o: part, lambda off: arrived.at[me_dp])
+        arrived[me_dp] = part[...]
         wait_all(recv_sem, phase, arrived)
-        for o in range(GROUP - 1):
-            mine = mine + arrived[o]
-        whole[me_dp] = mine
-        send_all("dp", phase + 1, lambda o: whole.at[me_dp], lambda off: whole.at[me_dp])
-        wait_all(recv_sem, phase + 1, whole)
-        return [
-            jnp.concatenate([whole[2 * k], whole[2 * k + 1]], axis=1) for k in range(REAL)
-        ]
-
-    def square_sums(rows):
-        total = jnp.zeros((1, 128), F32)
-        for k in range(REAL):
-            one = jnp.sum(rows[k] * rows[k], axis=1, keepdims=True)
-            total = jnp.where(iota((1, 128), 1) == k, one, total)
-        return total
-
-    def inverse_scale(own, arrived):
-        total = own
-        for o in range(GROUP - 1):
-            total = total + arrived[o]
-        diagonal = iota((8, 128), 0) == iota((8, 128), 1)
+        return unfold(sum_slots(arrived))
+
+    def send_squares(phase, whole, part, arrived):
+        squares = jnp.sum(whole * whole, axis=1, keepdims=True)
+        diagonal = iota((REAL, 128), 0) == iota((REAL, 128), 1)
+        part[...] = jnp.sum(jnp.where(diagonal, squares, 0.0), axis=0, keepdims=True)
+        send_all("cells", phase, lambda o: part, lambda off: arrived.at[me_cells])
+        arrived[me_cells] = part[...]
+
+    def inverse_scale(arrived):
+        total = sum_slots(arrived)
+        diagonal = iota((REAL, 128), 0) == iota((REAL, 128), 1)
         column = jnp.sum(jnp.where(diagonal, total, 0.0), axis=1, keepdims=True)
         return 1.0 / jnp.sqrt(column / cells_total + 1e-06)
 
     gradient(predicted, g1_s)
-    first = reduce_gradient(2, g1_s, g1_r, g1_a)
+    first = reduce_gradient(2, g1_s, g1_r)
+    send_squares(4, first, q1_s, q1_r)
 
     table = jnp.zeros((32 * REAL, 128), F32)
     for c in range(COMP):
         field = rc[c]
-        scaled = [(field * first[k]).astype(BF16) for k in range(REAL)]
+        scaled = [(field * first[k : k + 1]).astype(BF16) for k in range(REAL)]
         table = table + dot_nt(jnp.concatenate(scaled, axis=0), sc[c])
     spread = dot(split_halves(table * scale), is_source)
     change = jnp.concatenate(
@@ -262,66 +247,65 @@
         ],
         axis=0,
     )
-    half = n_data // 2
-    dl_s[...] = jnp.concatenate([change[:, :half], change[:, half:]], axis=0).astype(BF16)
-    q1_s[...] = square_sums(first)
-    send_all("cells", 4, lambda o: dl_s, lambda off: dl_r.at[off - 1])
-    send_all("cells", 5, lambda o: q1_s, lambda off: q1_r.at[off - 1])
-    wait_all(recv_sem, 5, q1_r)
-    inverse1 = inverse_scale(q1_s[...], q1_r)
-    wait_all(recv_sem, 4, dl_r)
-    total = dl_s[...].astype(F32)
-    for o in range(GROUP - 1):
-        total = total + dl_r[o].astype(F32)
-    change = jnp.concatenate([total[0:8], total[8:16]], axis=1)
+    dl_s[...] = fold(change).astype(BF16)
+    send_all("cells", 3, lambda o: dl_s, lambda off: dl_r.at[me_cells])
+    dl_r[me_cells] = dl_s[...]
+    wait_all(recv_sem, 4, q1_r)
+    inverse1 = inverse_scale(q1_r)
+    wait_all(recv_sem, 3, dl_r)
+    change = unfold(sum_slots(dl_r))
     gradient(predicted - 0.1 * (change * inverse1), g2_s)
-    second = reduce_gradient(6, g2_s, g2_r, g2_a)
-    q2_s[...] = square_sums(second)
-    send_all("cells", 8, lambda o: q2_s, lambda off: q2_r.at[off - 1])
-    velocity = jnp.concatenate(first, axis=0) * inverse1
+    velocity = first * inverse1
     base = (start - 0.1 * velocity) - 0.1 * (0.9 * velocity)
-    step = jnp.concatenate(second, axis=0)
-    wait_all(recv_sem, 8, q2_r)
-    out_ref[...] = base - 0.1 * (step * inverse_scale(q2_s[...], q2_r))
-
-    for phase, ref in enumerate((data_r, tab_r, g1_r, g1_a, dl_r, q1_r, g2_r, g2_a, q2_r)):
+    second = reduce_gradient(5, g2_s, g2_r)
+    send_squares(6, second, q2_s, q2_r)
+    wait_all(recv_sem, 6, q2_r)
+    out_ref[...] = base - 0.1 * (second * inverse_scale(q2_r))
+
+    for phase, ref in enumerate((data_r, tab_r, g1_r, dl_r, q1_r, g2_r, q2_r)):
         wait_all(send_sem, phase, ref)
 
 
 def on_device(source, receiver, source_index, receiver_index, observed, noise, huber, start):
     cells = start.shape[0]
     n_data = source_index.shape[0]
-    near = GROUP - 1
-    vmem = pl.BlockSpec(memory_space=pltpu.VMEM)
-    row = pltpu.VMEM((1, 128), F32)
-    rows = pltpu.VMEM((near, 1, 128), F32)
-    chunk = REAL * cells // GROUP
+    held = [
+        pltpu.VMEM((source.shape[0] * COMP, cells), BF16),
+        pltpu.VMEM((receiver.shape[0] * COMP, cells), BF16),
+        pltpu.VMEM((1, n_data), jnp.int32),
+        pltpu.VMEM((1, n_data), jnp.int32),
+        pltpu.VMEM((1, n_data), F32),
+        pltpu.VMEM((REAL, n_data), jnp.int32),
+        pltpu.SMEM((REAL,), jnp.int32),
+        pltpu.VMEM((cells // 128, 128), F32),
+    ]
+
+    def pair(shape, dtype):
+        return [pltpu.VMEM(shape, dtype), pltpu.VMEM((GROUP,) + shape, dtype)]
+
     return pl.pallas_call(
         functools.partial(body, cells * GROUP),
         out_shape=jax.ShapeDtypeStruct((REAL, cells), F32),
-        in_specs=[vmem] * 6 + [pl.BlockSpec(memory_space=pltpu.SMEM), vmem],
-        out_specs=vmem,
-        scratch_shapes=[
+        in_specs=[pl.BlockSpec(memory_space=pltpu.HBM)] * 8,
+        out_specs=pl.BlockSpec(memory_space=pltpu.VMEM),
+        scratch_shapes=held
+        + [
             pltpu.VMEM((COMP, 128, cells), BF16),
             pltpu.VMEM((COMP, 32, cells), F32),
+            pltpu.VMEM((REAL, cells), F32),
             pltpu.VMEM((4, 16, 128), F32),
             pltpu.VMEM((GROUP, 16, 128), F32),
-            pltpu.VMEM((2, 8, 128), F32),
-            pltpu.VMEM((near, 2, 8, 128), F32),
-            pltpu.VMEM((GROUP, 1, chunk), F32),
-            pltpu.VMEM((near, 1, chunk), F32),
-            pltpu.VMEM((GROUP, 1, chunk), F32),
-            pltpu.VMEM((16, n_data // 2), BF16),
-            pltpu.VMEM((near, 16, n_data // 2), BF16),
-            row,
-            rows,
-            pltpu.VMEM((GROUP, 1, chunk), F32),
-            pltpu.VMEM((near, 1, chunk), F32),
-            pltpu.VMEM((GROUP, 1, chunk), F32),
-            row,
-            rows,
-            pltpu.SemaphoreType.DMA((9,)),
-            pltpu.SemaphoreType.DMA((9,)),
+        ]
+        + pair((2, 8, 128), F32)
+        + pair((16, cells // 2), BF16)
+        + pair((16, n_data // 2), BF16)
+        + pair((1, 128), F32)
+        + pair((16, cells // 2), BF16)
+        + pair((1, 128), F32)
+        + [
+            pltpu.SemaphoreType.DMA((7,)),
+            pltpu.SemaphoreType.DMA((7,)),
+            pltpu.SemaphoreType.DMA((8,)),
         ],
         compiler_params=pltpu.CompilerParams(collective_id=0, has_side_effects=True),
     )(
@@ -332,7 +316,7 @@
         observed.reshape(1, n_data),
         noise,
         huber,
-        start.reshape(1, cells),
+        start.reshape(-1, 128),
     )
 
 

time: 56.5 us -> 46.3 us (0.82)
  Pallas kernels: 53.7 us -> 44.8 us
  local copies, waits for them, and re-layouts: 2.61 us -> 1.35 us
    pallas_call x1, Pallas kernels: 53.7 us -> 44.8 us  [on_device(): pl.pallas_call(functools.partial(body, cells * GROUP), out_shape=jax.Shap...]
    unnamed x3 -> x1, local copies, waits for them, and re-layouts: 2.03 us -> 1.35 us
    reshape x1 -> x0, local copies, waits for them, and re-layouts: 0.58 us -> none  [on_device(): start.reshape(1, cells)]
where the time goes in v2:
time: 46.3 us; the launch traced here: 46.2 us
  Pallas kernels  44.8 us (97%)
  local copies, waits for them, and re-layouts  1.35 us (3%)
    pallas_call x1, Pallas kernels, on_device(): pl.pallas_call(functools.partial(body, cells * GROUP), out_shape=jax.Shap...  44.8 us
    unnamed x1, local copies, waits for them, and re-layouts  1.35 us

profile of v2, /device:TPU:1, one launch (start us, length us, event | category | flops | bytes accessed | tf_op | source)
XLA Modules:
  0.0 46.2 jit_solution(13571149166271736557)
XLA Ops:
  0.0 44.8 %shard_map.82 = f32[8,768]{1,0:T(8,128)} custom-call(bf16[384,768]{1,0:T(8,128)(2,1)} %bitcast.6, bf16[256,768]{1,0:T(8,128)(2,1)} %bitcast.7, s32[1,512]{1,0:T(1,128)} %bitcast.9, s32[1,512]{1,0:T(1,128)} %bitcast.10, f32[1,512]{1,0:T(1,128)} %bitcast.11, s32[8,512]{1,0:T(8,128)} %refs_5_.1, s32[8]{0:T(128)} %refs_6_.1, f32[6,128]{1,0:T(8,128)} %bitcast.8), custom_call_target="tpu_custom_call" | custom-call | tf_op jit(solution)/shard_map/pallas_call | solution.py:286
  44.8 1.3 %copy.10 = f32[8,768]{1,0:T(8,128)} copy(f32[8,768]{1,0:T(8,128)} %shard_map.82) | data formatting | bytes 49152

commit v3 on v2

--- a/solution.py
+++ b/solution.py
@@ -285,7 +285,7 @@
 
     return pl.pallas_call(
         functools.partial(body, cells * GROUP),
-        out_shape=jax.ShapeDtypeStruct((REAL, cells), F32),
+        out_shape=pltpu.VMEM((REAL, cells), F32),
         in_specs=[pl.BlockSpec(memory_space=pltpu.HBM)] * 8,
         out_specs=pl.BlockSpec(memory_space=pltpu.VMEM),
         scratch_shapes=held

time: 46.3 us -> 44.9 us (0.970)
  local copies, waits for them, and re-layouts: 1.35 us -> 0.61 us
  Pallas kernels: 44.8 us -> 44.2 us
    unnamed x1, local copies, waits for them, and re-layouts: 1.35 us -> 0.61 us
    pallas_call x1, Pallas kernels: 44.8 us -> 44.2 us  [on_device(): pl.pallas_call(functools.partial(body, cells * GROUP), out_shape=pltpu.VM...]
where the time goes in v3:
time: 44.9 us; the launch traced here: 44.8 us
  Pallas kernels  44.2 us (98%)
  local copies, waits for them, and re-layouts  0.61 us (1%)
    pallas_call x1, Pallas kernels, on_device(): pl.pallas_call(functools.partial(body, cells * GROUP), out_shape=pltpu.VM...  44.2 us

profile of v3, /device:TPU:1, one launch (start us, length us, event | category | flops | bytes accessed | tf_op | source)
XLA Modules:
  0.0 44.8 jit_solution(7589903249479420215)
XLA Ops:
  0.0 44.2 %shard_map.82 = f32[8,768]{1,0:T(8,128)S(1)} custom-call(bf16[384,768]{1,0:T(8,128)(2,1)} %bitcast.6, bf16[256,768]{1,0:T(8,128)(2,1)} %bitcast.7, s32[1,512]{1,0:T(1,128)} %bitcast.9, s32[1,512]{1,0:T(1,128)} %bitcast.10, f32[1,512]{1,0:T(1,128)} %bitcast.11, s32[8,512]{1,0:T(8,128)} %refs_5_.1, s32[8]{0:T(128)} %refs_6_.1, f32[6,128]{1,0:T(8,128)} %bitcast.8), custom_call_target="tpu_custom_call" | custom-call | tf_op jit(solution)/shard_map/pallas_call | solution.py:286
  44.2 0.6 %copy.10 = f32[8,768]{1,0:T(8,128)} copy(f32[8,768]{1,0:T(8,128)S(1)} %shard_map.82) | data formatting | bytes 49152

commit v4 on v3

--- a/solution.py
+++ b/solution.py
@@ -13,6 +13,8 @@
 GROUP = 16
 COMP = 8
 REAL = 8
+SOURCES = 48
+RECEIVERS = 32
 MESH = pl.DeviceIdType.MESH
 FAR_FIRST = sorted(range(1, GROUP), key=lambda o: -min(o, GROUP - o))
 
@@ -40,8 +42,8 @@
 ):
     given, out_ref, held, refs = refs[:8], refs[8], refs[9:17], refs[17:]
     src_ref, rec_ref, sidx_ref, ridx_ref, obs_ref, noise_ref, huber_ref, start_ref = held
-    sc, rc, grad, data_s, data_r, tab_s, tab_r, g1_s, g1_r, dl_s, dl_r, q1_s, q1_r = refs[:13]
-    g2_s, g2_r, q2_s, q2_r, send_sem, recv_sem, load_sem = refs[13:]
+    sc, sf, rc, rk, ka, kd, data_s, data_r, tab_s, tab_r, g1_s, g1_r, dl_s, dl_r, q1_s, q1_r = refs[:16]
+    g2_s, g2_r, q2_s, q2_r, send_sem, recv_sem, load_sem = refs[16:]
     me_dp = lax.axis_index("dp")
     me_cells = lax.axis_index("cells")
     cells = src_ref.shape[1]
@@ -93,9 +95,11 @@
     loads[0].wait()
     zero_rows = jnp.zeros((16, cells), BF16)
     for chunk in range(3):
-        rows = dot(pick, src_ref[128 * chunk : 128 * chunk + 128, :]).astype(BF16)
+        rows = dot(pick, src_ref[128 * chunk : 128 * chunk + 128, :])
         for c in range(COMP):
             part = rows[16 * c : 16 * c + 16, :]
+            sf[c, 16 * chunk : 16 * chunk + 16, :] = part
+            part = part.astype(BF16)
             sc[c, 16 * chunk : 16 * chunk + 16, :] = part
             sc[c, 64 + 16 * chunk : 80 + 16 * chunk, :] = part
     for c in range(COMP):
@@ -115,9 +119,6 @@
     left = iota((8, 128), 1) < 64
     tab_s[0] = jnp.where(left, table[0:8], table[8:16])
     tab_s[1] = jnp.where(left, table[16:24], table[24:32])
-
-    pl.semaphore_wait(barrier, 2 * (GROUP - 1))
-    send_all("cells", 1, lambda o: tab_s, lambda off: tab_r.at[off - 1])
 
     for n in range(2, 7):
         loads[n].wait()
@@ -143,7 +144,26 @@
     for t in range(4):
         data_s[t, 0:8, :] = shifted[:, 128 * t : 128 * t + 128]
         data_s[t, 8:16, :] = moved[24:32, 128 * t : 128 * t + 128]
+    pl.semaphore_wait(barrier, 2 * (GROUP - 1))
+    send_all("cells", 1, lambda o: tab_s, lambda off: tab_r.at[off - 1])
     send_all("dp", 0, lambda o: data_s.at[o // 4], lambda off: data_r.at[off - 1])
+
+    signs = jnp.where(iota((COMP, cells), 0) % 2 == 0, scale, -scale)
+    for r in range(RECEIVERS):
+        rk[r] = rec_ref[COMP * r : COMP * r + COMP, :].astype(F32) * signs
+
+    def form(r, carry):
+        for n in range(cells // 128):
+            lanes = slice(128 * n, 128 * n + 128)
+            factors = rk[r, :, lanes]
+            rows = sf[0, :, lanes] * factors[0:1]
+            for c in range(1, COMP):
+                rows = rows + sf[c, :, lanes] * factors[c : c + 1]
+            ka[r, :, lanes] = rows.astype(BF16)
+        return carry
+
+    lax.fori_loop(0, RECEIVERS, form, 0)
+
     data_r[GROUP - 1] = data_s[me_dp // 4]
     wait_all(recv_sem, 0, data_r)
     quarter = iota((16, 128), 1) // 32
@@ -156,6 +176,11 @@
         tiles.append(tile)
     data = jnp.concatenate(tiles, axis=1)
     shifted = data[0:8]
+    column = jnp.transpose(data[8:16])
+    code = column[:, 1:2] * SOURCES + column[:, 0:1]
+    pairs = RECEIVERS * SOURCES
+    chosen = (iota((n_data, pairs), 1).astype(F32) == code).astype(F32).astype(BF16)
+    kd[...] = dot(chosen, ka[...].reshape(pairs, cells)).astype(BF16)
     source = data[8:9].astype(jnp.int32)
     receiver = data[9:10].astype(jnp.int32)
     is_source = (iota((128, n_data), 0) % 64 == source).astype(F32).astype(BF16)
@@ -192,24 +217,8 @@
         return parts[0]
 
     def gradient(predicted, out):
-        weighted = jnp.clip(predicted - shifted, -limit, limit).astype(BF16).astype(F32)
-        spread = [(weighted[k : k + 1, :] * is_receiver).astype(BF16) for k in range(REAL)]
-        pairs = split_halves(dot_nt(jnp.concatenate(spread, axis=0), is_source))
-        for b in range(cells // 256):
-            lanes = slice(256 * b, 256 * b + 256)
-            total = [jnp.zeros((8, 256), F32) for k in range(REAL)]
-            for c in range(COMP):
-                mixed = dot(pairs, sc[c, :, lanes])
-                field = rc[c, :, lanes]
-                for k in range(REAL):
-                    product = mixed[32 * k : 32 * k + 32] * field
-                    total[k] = total[k] + (
-                        (product[0:8] + product[8:16]) + (product[16:24] + product[24:32])
-                    )
-            for k in range(REAL):
-                grad[k : k + 1, lanes] = jnp.sum(total[k], axis=0, keepdims=True) * scale
-        whole = grad[...]
-        out[...] = fold(whole).astype(BF16)
+        weighted = jnp.clip(predicted - shifted, -limit, limit).astype(BF16)
+        out[...] = fold(dot(weighted, kd[...])).astype(BF16)
 
     def reduce_gradient(phase, part, arrived):
         send_all("dp", phase, lambda o: part, lambda off: arrived.at[me_dp])
@@ -234,19 +243,10 @@
     first = reduce_gradient(2, g1_s, g1_r)
     send_squares(4, first, q1_s, q1_r)
 
-    table = jnp.zeros((32 * REAL, 128), F32)
-    for c in range(COMP):
-        field = rc[c]
-        scaled = [(field * first[k : k + 1]).astype(BF16) for k in range(REAL)]
-        table = table + dot_nt(jnp.concatenate(scaled, axis=0), sc[c])
-    spread = dot(split_halves(table * scale), is_source)
-    change = jnp.concatenate(
-        [
-            jnp.sum(spread[32 * k : 32 * k + 32] * is_receiver, axis=0, keepdims=True)
-            for k in range(REAL)
-        ],
-        axis=0,
-    )
+    high = first.astype(BF16).astype(F32)
+    both = jnp.concatenate([high, first - high], axis=0).astype(BF16)
+    both = dot_nt(both, kd[...])
+    change = both[:REAL] + both[REAL:]
     dl_s[...] = fold(change).astype(BF16)
     send_all("cells", 3, lambda o: dl_s, lambda off: dl_r.at[me_cells])
     dl_r[me_cells] = dl_s[...]
@@ -291,8 +291,11 @@
         scratch_shapes=held
         + [
             pltpu.VMEM((COMP, 128, cells), BF16),
-            pltpu.VMEM((COMP, 32, cells), F32),
-            pltpu.VMEM((REAL, cells), F32),
+            pltpu.VMEM((COMP, SOURCES, cells), F32),
+            pltpu.VMEM((COMP, RECEIVERS, cells), F32),
+            pltpu.VMEM((RECEIVERS, COMP, cells), F32),
+            pltpu.VMEM((RECEIVERS, SOURCES, cells), BF16),
+            pltpu.VMEM((n_data, cells), BF16),
             pltpu.VMEM((4, 16, 128), F32),
             pltpu.VMEM((GROUP, 16, 128), F32),
         ]

time: 44.9 us -> 41.9 us (0.933)
  Pallas kernels: 44.2 us -> 41.2 us
    pallas_call x1, Pallas kernels: 44.2 us -> 41.2 us  [on_device(): pl.pallas_call(functools.partial(body, cells * GROUP), out_shape=pltpu.VM...]
where the time goes in v4:
time: 41.9 us; the launch traced here: 41.8 us
  Pallas kernels  41.2 us (98%)
  local copies, waits for them, and re-layouts  0.61 us (1%)
    pallas_call x1, Pallas kernels, on_device(): pl.pallas_call(functools.partial(body, cells * GROUP), out_shape=pltpu.VM...  41.2 us

profile of v4, /device:TPU:1, one launch (start us, length us, event | category | flops | bytes accessed | tf_op | source)
XLA Modules:
  0.0 41.8 jit_solution(9905402307221169105)
XLA Ops:
  0.0 41.2 %shard_map.82 = f32[8,768]{1,0:T(8,128)S(1)} custom-call(bf16[384,768]{1,0:T(8,128)(2,1)} %bitcast.6, bf16[256,768]{1,0:T(8,128)(2,1)} %bitcast.7, s32[1,512]{1,0:T(1,128)} %bitcast.9, s32[1,512]{1,0:T(1,128)} %bitcast.10, f32[1,512]{1,0:T(1,128)} %bitcast.11, s32[8,512]{1,0:T(8,128)} %refs_5_.1, s32[8]{0:T(128)} %refs_6_.1, f32[6,128]{1,0:T(8,128)} %bitcast.8), custom_call_target="tpu_custom_call" | custom-call | tf_op jit(solution)/shard_map/pallas_call | solution.py:286
  41.2 0.6 %copy.10 = f32[8,768]{1,0:T(8,128)} copy(f32[8,768]{1,0:T(8,128)S(1)} %shard_map.82) | data formatting | bytes 49152

commit v5 on v4

--- a/solution.py
+++ b/solution.py
@@ -42,8 +42,8 @@
 ):
     given, out_ref, held, refs = refs[:8], refs[8], refs[9:17], refs[17:]
     src_ref, rec_ref, sidx_ref, ridx_ref, obs_ref, noise_ref, huber_ref, start_ref = held
-    sc, sf, rc, rk, ka, kd, data_s, data_r, tab_s, tab_r, g1_s, g1_r, dl_s, dl_r, q1_s, q1_r = refs[:16]
-    g2_s, g2_r, q2_s, q2_r, send_sem, recv_sem, load_sem = refs[16:]
+    sf, rk, ka, kd, oh, data_s, data_r, tab_s, tab_r, g1_s, g1_r, dl_s, dl_r, q1_s, q1_r = refs[:15]
+    g2_s, g2_r, q2_s, q2_r, send_sem, recv_sem, load_sem = refs[15:]
     me_dp = lax.axis_index("dp")
     me_cells = lax.axis_index("cells")
     cells = src_ref.shape[1]
@@ -56,16 +56,20 @@
 
     barrier = pltpu.get_barrier_semaphore()
 
-    for offset in FAR_FIRST:
-        for axis in ("cells", "dp"):
+    def greet(axis, offsets):
+        for offset in offsets:
             pl.semaphore_signal(
                 barrier, inc=1, device_id={axis: peer(axis, offset)}, device_id_type=MESH
             )
+
+    greet("cells", FAR_FIRST[:8])
     loads = [
         pltpu.make_async_copy(a, b, load_sem.at[n]) for n, (a, b) in enumerate(zip(given, held))
     ]
-    for n in (1, 7, 0, 2, 3, 4, 5, 6):
+    for n in (3, 2, 4, 5, 1, 7, 0, 6):
         loads[n].start()
+    greet("cells", FAR_FIRST[8:])
+    greet("dp", FAR_FIRST)
 
     def send_all(axis, phase, src_of, dst_of):
         for offset in FAR_FIRST:
@@ -82,43 +86,6 @@
     def wait_all(sem, phase, ref):
         part = ref.at[pl.ds(0, GROUP - 1)]
         pltpu.make_async_copy(part, part, sem.at[phase]).wait()
-
-    pick = (
-        (iota((128, 128), 0) % 16) * COMP + iota((128, 128), 0) // 16 == iota((128, 128), 1)
-    ).astype(F32).astype(BF16)
-    loads[1].wait()
-    for chunk in range(2):
-        rows = dot(pick, rec_ref[128 * chunk : 128 * chunk + 128, :])
-        for c in range(COMP):
-            part = rows[16 * c : 16 * c + 16, :]
-            rc[c, 16 * chunk : 16 * chunk + 16, :] = part if c % 2 == 0 else -part
-    loads[0].wait()
-    zero_rows = jnp.zeros((16, cells), BF16)
-    for chunk in range(3):
-        rows = dot(pick, src_ref[128 * chunk : 128 * chunk + 128, :])
-        for c in range(COMP):
-            part = rows[16 * c : 16 * c + 16, :]
-            sf[c, 16 * chunk : 16 * chunk + 16, :] = part
-            part = part.astype(BF16)
-            sc[c, 16 * chunk : 16 * chunk + 16, :] = part
-            sc[c, 64 + 16 * chunk : 80 + 16 * chunk, :] = part
-    for c in range(COMP):
-        sc[c, 48:64, :] = zero_rows
-        sc[c, 112:128, :] = zero_rows
-
-    loads[7].wait()
-    start = jnp.concatenate([start_ref[n : n + 1, :] for n in range(cells // 128)], axis=1)
-    start_half = start.astype(BF16).astype(F32)
-    table = jnp.zeros((64, 128), F32)
-    for c in range(COMP):
-        exact = rc[c] * start_half
-        high = exact.astype(BF16)
-        low = (exact - high.astype(F32)).astype(BF16)
-        table = table + dot_nt(jnp.concatenate([high, low], axis=0), sc[c])
-    table = (table[0:32] + table[32:64]) * scale
-    left = iota((8, 128), 1) < 64
-    tab_s[0] = jnp.where(left, table[0:8], table[8:16])
-    tab_s[1] = jnp.where(left, table[16:24], table[24:32])
 
     for n in range(2, 7):
         loads[n].wait()
@@ -144,9 +111,46 @@
     for t in range(4):
         data_s[t, 0:8, :] = shifted[:, 128 * t : 128 * t + 128]
         data_s[t, 8:16, :] = moved[24:32, 128 * t : 128 * t + 128]
+
+    for n in (1, 7):
+        loads[n].wait()
+    start = jnp.concatenate([start_ref[n : n + 1, :] for n in range(cells // 128)], axis=1)
+    exact = rec_ref[...].astype(F32) * start.astype(BF16).astype(F32)
+    high = exact.astype(BF16)
+    low = (exact - high.astype(F32)).astype(BF16)
+    loads[0].wait()
+    cross = dot_nt(high, src_ref[...]) + dot_nt(low, src_ref[...])
+    shape = (COMP, SOURCES * COMP)
+    odd = iota(shape, 0) % 2
+    keep = jnp.where(iota(shape, 1) % COMP == iota(shape, 0), 1.0 - 2.0 * odd.astype(F32), 0.0)
+    table = jnp.concatenate(
+        [
+            jnp.sum(cross[COMP * r : COMP * r + COMP] * keep, axis=0, keepdims=True)
+            for r in range(RECEIVERS)
+        ],
+        axis=0,
+    )
+    high = table.astype(BF16)
+    low = (table - high.astype(F32)).astype(BF16)
+    shape = (SOURCES * COMP, 128)
+    group = (iota(shape, 0) // COMP == iota(shape, 1) % 64).astype(F32).astype(BF16)
+    table = dot(jnp.concatenate([high, low], axis=0), group)
+    table = (table[:RECEIVERS] + table[RECEIVERS:]) * scale
+    left = iota((8, 128), 1) < 64
+    tab_s[0] = jnp.where(left, table[0:8], table[8:16])
+    tab_s[1] = jnp.where(left, table[16:24], table[24:32])
+
     pl.semaphore_wait(barrier, 2 * (GROUP - 1))
+    send_all("dp", 0, lambda o: data_s.at[o // 4], lambda off: data_r.at[off - 1])
     send_all("cells", 1, lambda o: tab_s, lambda off: tab_r.at[off - 1])
-    send_all("dp", 0, lambda o: data_s.at[o // 4], lambda off: data_r.at[off - 1])
+
+    pick = (
+        (iota((128, 128), 0) % 16) * COMP + iota((128, 128), 0) // 16 == iota((128, 128), 1)
+    ).astype(F32).astype(BF16)
+    for chunk in range(3):
+        rows = dot(pick, src_ref[128 * chunk : 128 * chunk + 128, :])
+        for c in range(COMP):
+            sf[c, 16 * chunk : 16 * chunk + 16, :] = rows[16 * c : 16 * c + 16, :]
 
     signs = jnp.where(iota((COMP, cells), 0) % 2 == 0, scale, -scale)
     for r in range(RECEIVERS):
@@ -179,8 +183,7 @@
     column = jnp.transpose(data[8:16])
     code = column[:, 1:2] * SOURCES + column[:, 0:1]
     pairs = RECEIVERS * SOURCES
-    chosen = (iota((n_data, pairs), 1).astype(F32) == code).astype(F32).astype(BF16)
-    kd[...] = dot(chosen, ka[...].reshape(pairs, cells)).astype(BF16)
+    oh[...] = (iota((n_data, pairs), 1).astype(F32) == code).astype(F32).astype(BF16)
     source = data[8:9].astype(jnp.int32)
     receiver = data[9:10].astype(jnp.int32)
     is_source = (iota((128, n_data), 0) % 64 == source).astype(F32).astype(BF16)
@@ -216,13 +219,18 @@
             parts = [a + b for a, b in zip(parts[::2], parts[1::2])]
         return parts[0]
 
-    def gradient(predicted, out):
-        weighted = jnp.clip(predicted - shifted, -limit, limit).astype(BF16)
-        out[...] = fold(dot(weighted, kd[...])).astype(BF16)
-
-    def reduce_gradient(phase, part, arrived):
+    def two_parts(x):
+        high = x.astype(BF16).astype(F32)
+        return jnp.concatenate([high, x - high], axis=0).astype(BF16)
+
+    def weigh(predicted):
+        return jnp.clip(predicted - shifted, -limit, limit).astype(BF16)
+
+    def reduce_gradient(phase, whole, part, arrived, meanwhile):
+        part[...] = fold(whole).astype(BF16)
         send_all("dp", phase, lambda o: part, lambda off: arrived.at[me_dp])
         arrived[me_dp] = part[...]
+        meanwhile()
         wait_all(recv_sem, phase, arrived)
         return unfold(sum_slots(arrived))
 
@@ -239,13 +247,14 @@
         column = jnp.sum(jnp.where(diagonal, total, 0.0), axis=1, keepdims=True)
         return 1.0 / jnp.sqrt(column / cells_total + 1e-06)
 
-    gradient(predicted, g1_s)
-    first = reduce_gradient(2, g1_s, g1_r)
+    def pick_rows():
+        kd[...] = dot(oh[...], ka[...].reshape(pairs, cells)).astype(BF16)
+
+    both = dot(two_parts(dot(weigh(predicted), oh[...])), ka[...].reshape(pairs, cells))
+    first = reduce_gradient(2, both[:REAL] + both[REAL:], g1_s, g1_r, pick_rows)
     send_squares(4, first, q1_s, q1_r)
 
-    high = first.astype(BF16).astype(F32)
-    both = jnp.concatenate([high, first - high], axis=0).astype(BF16)
-    both = dot_nt(both, kd[...])
+    both = dot_nt(two_parts(first), kd[...])
     change = both[:REAL] + both[REAL:]
     dl_s[...] = fold(change).astype(BF16)
     send_all("cells", 3, lambda o: dl_s, lambda off: dl_r.at[me_cells])
@@ -254,11 +263,11 @@
     inverse1 = inverse_scale(q1_r)
     wait_all(recv_sem, 3, dl_r)
     change = unfold(sum_slots(dl_r))
-    gradient(predicted - 0.1 * (change * inverse1), g2_s)
+    whole = dot(weigh(predicted - 0.1 * (change * inverse1)), kd[...])
+    second = reduce_gradient(5, whole, g2_s, g2_r, lambda: None)
+    send_squares(6, second, q2_s, q2_r)
     velocity = first * inverse1
     base = (start - 0.1 * velocity) - 0.1 * (0.9 * velocity)
-    second = reduce_gradient(5, g2_s, g2_r)
-    send_squares(6, second, q2_s, q2_r)
     wait_all(recv_sem, 6, q2_r)
     out_ref[...] = base - 0.1 * (second * inverse_scale(q2_r))
 
@@ -290,12 +299,11 @@
         out_specs=pl.BlockSpec(memory_space=pltpu.VMEM),
         scratch_shapes=held
         + [
-            pltpu.VMEM((COMP, 128, cells), BF16),
             pltpu.VMEM((COMP, SOURCES, cells), F32),
-            pltpu.VMEM((COMP, RECEIVERS, cells), F32),
             pltpu.VMEM((RECEIVERS, COMP, cells), F32),
             pltpu.VMEM((RECEIVERS, SOURCES, cells), BF16),
             pltpu.VMEM((n_data, cells), BF16),
+            pltpu.VMEM((n_data, RECEIVERS * SOURCES), BF16),
             pltpu.VMEM((4, 16, 128), F32),
             pltpu.VMEM((GROUP, 16, 128), F32),
         ]

time: 41.9 us -> 41.2 us (0.983)
  Pallas kernels: 41.2 us -> 40.5 us
    pallas_call x1, Pallas kernels: 41.2 us -> 40.5 us  [on_device(): pl.pallas_call(functools.partial(body, cells * GROUP), out_shape=pltpu.VM...]
where the time goes in v5:
time: 41.2 us; the launch traced here: 41.1 us
  Pallas kernels  40.5 us (98%)
  local copies, waits for them, and re-layouts  0.61 us (1%)
    pallas_call x1, Pallas kernels, on_device(): pl.pallas_call(functools.partial(body, cells * GROUP), out_shape=pltpu.VM...  40.5 us

profile of v5, /device:TPU:1, one launch (start us, length us, event | category | flops | bytes accessed | tf_op | source)
XLA Modules:
  0.0 41.1 jit_solution(6638862928742443092)
XLA Ops:
  0.0 40.5 %shard_map.82 = f32[8,768]{1,0:T(8,128)S(1)} custom-call(bf16[384,768]{1,0:T(8,128)(2,1)} %bitcast.6, bf16[256,768]{1,0:T(8,128)(2,1)} %bitcast.7, s32[1,512]{1,0:T(1,128)} %bitcast.9, s32[1,512]{1,0:T(1,128)} %bitcast.10, f32[1,512]{1,0:T(1,128)} %bitcast.11, s32[8,512]{1,0:T(8,128)} %refs_5_.1, s32[8]{0:T(128)} %refs_6_.1, f32[6,128]{1,0:T(8,128)} %bitcast.8), custom_call_target="tpu_custom_call" | custom-call | tf_op jit(solution)/shard_map/pallas_call | solution.py:295
  40.5 0.6 %copy.10 = f32[8,768]{1,0:T(8,128)} copy(f32[8,768]{1,0:T(8,128)S(1)} %shard_map.82) | data formatting | bytes 49152

commit v6 on v5

--- a/solution.py
+++ b/solution.py
@@ -16,7 +16,21 @@
 SOURCES = 48
 RECEIVERS = 32
 MESH = pl.DeviceIdType.MESH
-FAR_FIRST = sorted(range(1, GROUP), key=lambda o: -min(o, GROUP - o))
+
+
+def hops(step, ring):
+    return min(step, ring - step)
+
+
+CELLS_ORDER = sorted(
+    ((step, flip) for step in range(8) for flip in range(2) if step or flip),
+    key=lambda p: -(hops(p[0], 8) + 2 * p[1]),
+)
+DP_ORDER = sorted(
+    ((y, x, core) for y in range(4) for x in range(2) for core in range(2) if y or x or core),
+    key=lambda p: -((0, 1, 2, 1)[p[0]] + p[1] + 0.1 * p[2]),
+)
+ORDERS = {"cells": CELLS_ORDER, "dp": DP_ORDER}
 
 
 def iota(shape, axis):
@@ -50,38 +64,62 @@
     n_data = sidx_ref.shape[1]
     scale = 0.2 / math.sqrt(COMP * cells_total)
 
-    def peer(axis, offset):
-        me = me_dp if axis == "dp" else me_cells
-        return lax.rem(me + offset, GROUP)
+    def flipped(value, bit, flip):
+        return lax.rem(value // bit + flip, 2) * bit
+
+    def peer(axis, pattern):
+        if axis == "cells":
+            step, flip = pattern
+            return 2 * lax.rem(me_cells // 2 + step, 8) + flipped(me_cells, 1, flip)
+        y, x, core = pattern
+        me = me_dp
+        return (
+            flipped(me, 8, y // 2) + flipped(me, 4, y % 2) + flipped(me, 2, x) + flipped(me, 1, core)
+        )
 
     barrier = pltpu.get_barrier_semaphore()
 
-    def greet(axis, offsets):
-        for offset in offsets:
+    def greet(axis, patterns):
+        for pattern in patterns:
             pl.semaphore_signal(
-                barrier, inc=1, device_id={axis: peer(axis, offset)}, device_id_type=MESH
+                barrier, inc=1, device_id={axis: peer(axis, pattern)}, device_id_type=MESH
             )
 
-    greet("cells", FAR_FIRST[:8])
+    greet("cells", CELLS_ORDER[:8])
     loads = [
         pltpu.make_async_copy(a, b, load_sem.at[n]) for n, (a, b) in enumerate(zip(given, held))
     ]
     for n in (3, 2, 4, 5, 1, 7, 0, 6):
         loads[n].start()
-    greet("cells", FAR_FIRST[8:])
-    greet("dp", FAR_FIRST)
-
-    def send_all(axis, phase, src_of, dst_of):
-        for offset in FAR_FIRST:
-            other = peer(axis, offset)
+    greet("cells", CELLS_ORDER[8:])
+    greet("dp", DP_ORDER)
+
+    def send_all(axis, phase, src_of, arrived):
+        mine = me_cells if axis == "cells" else me_dp
+        for pattern in ORDERS[axis]:
+            other = peer(axis, pattern)
             pltpu.make_async_remote_copy(
                 src_ref=src_of(other),
-                dst_ref=dst_of(offset),
+                dst_ref=arrived.at[mine],
                 send_sem=send_sem.at[phase],
                 recv_sem=recv_sem.at[phase],
                 device_id={axis: other},
                 device_id_type=MESH,
             ).start()
+
+    def fold(x):
+        half = x.shape[1] // 2
+        return jnp.concatenate([x[:, :half], x[:, half:]], axis=0)
+
+    def unfold(x):
+        half = x.shape[0] // 2
+        return jnp.concatenate([x[:half], x[half:]], axis=1)
+
+    def sum_slots(arrived):
+        parts = [arrived[o].astype(F32) for o in range(GROUP)]
+        while len(parts) > 1:
+            parts = [a + b for a, b in zip(parts[::2], parts[1::2])]
+        return parts[0]
 
     def wait_all(sem, phase, ref):
         part = ref.at[pl.ds(0, GROUP - 1)]
@@ -141,8 +179,8 @@
     tab_s[1] = jnp.where(left, table[16:24], table[24:32])
 
     pl.semaphore_wait(barrier, 2 * (GROUP - 1))
-    send_all("dp", 0, lambda o: data_s.at[o // 4], lambda off: data_r.at[off - 1])
-    send_all("cells", 1, lambda o: tab_s, lambda off: tab_r.at[off - 1])
+    send_all("dp", 0, lambda o: data_s.at[o // 4], data_r)
+    send_all("cells", 1, lambda o: tab_s, tab_r)
 
     pick = (
         (iota((128, 128), 0) % 16) * COMP + iota((128, 128), 0) // 16 == iota((128, 128), 1)
@@ -168,15 +206,15 @@
 
     lax.fori_loop(0, RECEIVERS, form, 0)
 
-    data_r[GROUP - 1] = data_s[me_dp // 4]
+    data_r[me_dp] = data_s[me_dp // 4]
+    tab_r[me_cells] = tab_s[...]
     wait_all(recv_sem, 0, data_r)
     quarter = iota((16, 128), 1) // 32
     tiles = []
     for t in range(4):
         tile = data_r[4 * t]
-        for o in range(4 * t + 2, 4 * t + 5):
-            here = lax.rem(2 * me_dp + 32 - o, 4)
-            tile = jnp.where(quarter == here, data_r[o - 1], tile)
+        for sender in range(4 * t + 1, 4 * t + 4):
+            tile = jnp.where(quarter == lax.rem(me_dp + sender, 4), data_r[sender], tile)
         tiles.append(tile)
     data = jnp.concatenate(tiles, axis=1)
     shifted = data[0:8]
@@ -193,9 +231,7 @@
         limit = jnp.where(row8 == k, huber_ref[k].astype(F32) / 16.0, limit)
 
     wait_all(recv_sem, 1, tab_r)
-    packed = tab_s[...]
-    for o in range(GROUP - 1):
-        packed = packed + tab_r[o]
+    packed = sum_slots(tab_r)
     rows = []
     for t in range(2):
         here = packed[t]
@@ -205,20 +241,6 @@
     spread = dot(split_halves(jnp.concatenate(rows, axis=0)), is_source)
     predicted = jnp.sum(spread * is_receiver, axis=0, keepdims=True)
 
-    def fold(x):
-        half = x.shape[1] // 2
-        return jnp.concatenate([x[:, :half], x[:, half:]], axis=0)
-
-    def unfold(x):
-        half = x.shape[0] // 2
-        return jnp.concatenate([x[:half], x[half:]], axis=1)
-
-    def sum_slots(arrived):
-        parts = [arrived[o].astype(F32) for o in range(GROUP)]
-        while len(parts) > 1:
-            parts = [a + b for a, b in zip(parts[::2], parts[1::2])]
-        return parts[0]
-
     def two_parts(x):
         high = x.astype(BF16).astype(F32)
         return jnp.concatenate([high, x - high], axis=0).astype(BF16)
@@ -228,7 +250,7 @@
 
     def reduce_gradient(phase, whole, part, arrived, meanwhile):
         part[...] = fold(whole).astype(BF16)
-        send_all("dp", phase, lambda o: part, lambda off: arrived.at[me_dp])
+        send_all("dp", phase, lambda o: part, arrived)
         arrived[me_dp] = part[...]
         meanwhile()
         wait_all(recv_sem, phase, arrived)
@@ -238,7 +260,7 @@
         squares = jnp.sum(whole * whole, axis=1, keepdims=True)
         diagonal = iota((REAL, 128), 0) == iota((REAL, 128), 1)
         part[...] = jnp.sum(jnp.where(diagonal, squares, 0.0), axis=0, keepdims=True)
-        send_all("cells", phase, lambda o: part, lambda off: arrived.at[me_cells])
+        send_all("cells", phase, lambda o: part, arrived)
         arrived[me_cells] = part[...]
 
     def inverse_scale(arrived):
@@ -257,7 +279,7 @@
     both = dot_nt(two_parts(first), kd[...])
     change = both[:REAL] + both[REAL:]
     dl_s[...] = fold(change).astype(BF16)
-    send_all("cells", 3, lambda o: dl_s, lambda off: dl_r.at[me_cells])
+    send_all("cells", 3, lambda o: dl_s, dl_r)
     dl_r[me_cells] = dl_s[...]
     wait_all(recv_sem, 4, q1_r)
     inverse1 = inverse_scale(q1_r)

time: 41.2 us -> 40 us (0.971)
  Pallas kernels: 40.5 us -> 39.2 us
    pallas_call x1, Pallas kernels: 40.5 us -> 39.2 us  [on_device(): pl.pallas_call(functools.partial(body, cells * GROUP), out_shape=pltpu.VM...]
where the time goes in v6:
time: 40 us; the launch traced here: 39.9 us
  Pallas kernels  39.2 us (98%)
  local copies, waits for them, and re-layouts  0.61 us (2%)
    pallas_call x1, Pallas kernels, on_device(): pl.pallas_call(functools.partial(body, cells * GROUP), out_shape=pltpu.VM...  39.2 us

profile of v6, /device:TPU:1, one launch (start us, length us, event | category | flops | bytes accessed | tf_op | source)
XLA Modules:
  0.0 39.9 jit_solution(8670462648729177991)
XLA Ops:
  0.0 39.2 %shard_map.82 = f32[8,768]{1,0:T(8,128)S(1)} custom-call(bf16[384,768]{1,0:T(8,128)(2,1)} %bitcast.6, bf16[256,768]{1,0:T(8,128)(2,1)} %bitcast.7, s32[1,512]{1,0:T(1,128)} %bitcast.9, s32[1,512]{1,0:T(1,128)} %bitcast.10, f32[1,512]{1,0:T(1,128)} %bitcast.11, s32[8,512]{1,0:T(8,128)} %refs_5_.1, s32[8]{0:T(128)} %refs_6_.1, f32[6,128]{1,0:T(8,128)} %bitcast.8), custom_call_target="tpu_custom_call" | custom-call | tf_op jit(solution)/shard_map/pallas_call | solution.py:317
  39.3 0.6 %copy.10 = f32[8,768]{1,0:T(8,128)} copy(f32[8,768]{1,0:T(8,128)S(1)} %shard_map.82) | data formatting | bytes 49152

commit v7 on v6

--- a/solution.py
+++ b/solution.py
@@ -146,9 +146,12 @@
     )
     moved = dot_nt(jnp.concatenate([high, middle, low, index_rows], axis=0).astype(BF16), move)
     shifted = moved[0:8] + moved[8:16] + moved[16:24]
+    quarter = iota((8, 128), 1) // 32
     for t in range(4):
-        data_s[t, 0:8, :] = shifted[:, 128 * t : 128 * t + 128]
-        data_s[t, 8:16, :] = moved[24:32, 128 * t : 128 * t + 128]
+        lanes = slice(128 * t, 128 * t + 128)
+        beside = pltpu.roll(moved[24:32, lanes], 32, 1)
+        for o in range(4 * t, 4 * t + 4):
+            data_s[o] = jnp.where(quarter == lax.rem(me_dp + o, 4), shifted[:, lanes], beside)
 
     for n in (1, 7):
         loads[n].wait()
@@ -175,12 +178,13 @@
     table = dot(jnp.concatenate([high, low], axis=0), group)
     table = (table[:RECEIVERS] + table[RECEIVERS:]) * scale
     left = iota((8, 128), 1) < 64
-    tab_s[0] = jnp.where(left, table[0:8], table[8:16])
-    tab_s[1] = jnp.where(left, table[16:24], table[24:32])
+    tab_s[...] = jnp.concatenate(
+        [jnp.where(left, table[0:8], table[8:16]), jnp.where(left, table[16:24], table[24:32])], axis=0
+    ).astype(BF16)
 
     pl.semaphore_wait(barrier, 2 * (GROUP - 1))
-    send_all("dp", 0, lambda o: data_s.at[o // 4], data_r)
     send_all("cells", 1, lambda o: tab_s, tab_r)
+    send_all("dp", 0, lambda o: data_s.at[o], data_r)
 
     pick = (
         (iota((128, 128), 0) % 16) * COMP + iota((128, 128), 0) // 16 == iota((128, 128), 1)
@@ -206,24 +210,26 @@
 
     lax.fori_loop(0, RECEIVERS, form, 0)
 
-    data_r[me_dp] = data_s[me_dp // 4]
+    data_r[me_dp] = data_s[me_dp]
     tab_r[me_cells] = tab_s[...]
     wait_all(recv_sem, 0, data_r)
-    quarter = iota((16, 128), 1) // 32
-    tiles = []
+    values, indices = [], []
     for t in range(4):
-        tile = data_r[4 * t]
+        tile = beside = data_r[4 * t]
         for sender in range(4 * t + 1, 4 * t + 4):
-            tile = jnp.where(quarter == lax.rem(me_dp + sender, 4), data_r[sender], tile)
-        tiles.append(tile)
-    data = jnp.concatenate(tiles, axis=1)
-    shifted = data[0:8]
-    column = jnp.transpose(data[8:16])
+            here = data_r[sender]
+            tile = jnp.where(quarter == lax.rem(me_dp + sender, 4), here, tile)
+            beside = jnp.where(quarter == lax.rem(me_dp + sender + 1, 4), here, beside)
+        values.append(tile)
+        indices.append(pltpu.roll(beside, 96, 1))
+    shifted = jnp.concatenate(values, axis=1)
+    indices = jnp.concatenate(indices, axis=1)
+    column = jnp.transpose(indices)
     code = column[:, 1:2] * SOURCES + column[:, 0:1]
     pairs = RECEIVERS * SOURCES
     oh[...] = (iota((n_data, pairs), 1).astype(F32) == code).astype(F32).astype(BF16)
-    source = data[8:9].astype(jnp.int32)
-    receiver = data[9:10].astype(jnp.int32)
+    source = indices[0:1].astype(jnp.int32)
+    receiver = indices[1:2].astype(jnp.int32)
     is_source = (iota((128, n_data), 0) % 64 == source).astype(F32).astype(BF16)
     is_receiver = (iota((32, n_data), 0) == receiver).astype(F32)
     limit = jnp.zeros((REAL, n_data), F32)
@@ -234,7 +240,7 @@
     packed = sum_slots(tab_r)
     rows = []
     for t in range(2):
-        here = packed[t]
+        here = packed[8 * t : 8 * t + 8]
         turned = pltpu.roll(here, 64, 1)
         rows.append(jnp.where(left, here, turned))
         rows.append(jnp.where(left, turned, here))
@@ -326,10 +332,10 @@
             pltpu.VMEM((RECEIVERS, SOURCES, cells), BF16),
             pltpu.VMEM((n_data, cells), BF16),
             pltpu.VMEM((n_data, RECEIVERS * SOURCES), BF16),
-            pltpu.VMEM((4, 16, 128), F32),
-            pltpu.VMEM((GROUP, 16, 128), F32),
+            pltpu.VMEM((GROUP, 8, 128), F32),
+            pltpu.VMEM((GROUP, 8, 128), F32),
         ]
-        + pair((2, 8, 128), F32)
+        + pair((16, 128), BF16)
         + pair((16, cells // 2), BF16)
         + pair((16, n_data // 2), BF16)
         + pair((1, 128), F32)

time: 40 us -> 39.4 us (0.985)
  Pallas kernels: 39.2 us -> 38.7 us
    pallas_call x1, Pallas kernels: 39.2 us -> 38.7 us  [on_device(): pl.pallas_call(functools.partial(body, cells * GROUP), out_shape=pltpu.VM...]
where the time goes in v7:
time: 39.4 us; the launch traced here: 39.3 us
  Pallas kernels  38.7 us (98%)
  local copies, waits for them, and re-layouts  0.61 us (2%)
    pallas_call x1, Pallas kernels, on_device(): pl.pallas_call(functools.partial(body, cells * GROUP), out_shape=pltpu.VM...  38.7 us

profile of v7, /device:TPU:1, one launch (start us, length us, event | category | flops | bytes accessed | tf_op | source)
XLA Modules:
  0.0 39.3 jit_solution(17495025582204812115)
XLA Ops:
  0.0 38.7 %shard_map.82 = f32[8,768]{1,0:T(8,128)S(1)} custom-call(bf16[384,768]{1,0:T(8,128)(2,1)} %bitcast.6, bf16[256,768]{1,0:T(8,128)(2,1)} %bitcast.7, s32[1,512]{1,0:T(1,128)} %bitcast.9, s32[1,512]{1,0:T(1,128)} %bitcast.10, f32[1,512]{1,0:T(1,128)} %bitcast.11, s32[8,512]{1,0:T(8,128)} %refs_5_.1, s32[8]{0:T(128)} %refs_6_.1, f32[6,128]{1,0:T(8,128)} %bitcast.8), custom_call_target="tpu_custom_call" | custom-call | tf_op jit(solution)/shard_map/pallas_call | solution.py:323
  38.7 0.6 %copy.10 = f32[8,768]{1,0:T(8,128)} copy(f32[8,768]{1,0:T(8,128)S(1)} %shard_map.82) | data formatting | bytes 49152

commit v8 on v7

--- a/solution.py
+++ b/solution.py
@@ -15,7 +15,7 @@
 REAL = 8
 SOURCES = 48
 RECEIVERS = 32
-MESH = pl.DeviceIdType.MESH
+LOGICAL = pl.DeviceIdType.LOGICAL
 
 
 def hops(step, ring):
@@ -30,7 +30,6 @@
     ((y, x, core) for y in range(4) for x in range(2) for core in range(2) if y or x or core),
     key=lambda p: -((0, 1, 2, 1)[p[0]] + p[1] + 0.1 * p[2]),
 )
-ORDERS = {"cells": CELLS_ORDER, "dp": DP_ORDER}
 
 
 def iota(shape, axis):
@@ -77,34 +76,36 @@
             flipped(me, 8, y // 2) + flipped(me, 4, y % 2) + flipped(me, 2, x) + flipped(me, 1, core)
         )
 
+    peers = {
+        "cells": [(peer("cells", p), me_dp * GROUP + peer("cells", p)) for p in CELLS_ORDER],
+        "dp": [(peer("dp", p), peer("dp", p) * GROUP + me_cells) for p in DP_ORDER],
+    }
+
     barrier = pltpu.get_barrier_semaphore()
 
     def greet(axis, patterns):
-        for pattern in patterns:
-            pl.semaphore_signal(
-                barrier, inc=1, device_id={axis: peer(axis, pattern)}, device_id_type=MESH
-            )
-
-    greet("cells", CELLS_ORDER[:8])
+        for _, device in patterns:
+            pl.semaphore_signal(barrier, inc=1, device_id=device, device_id_type=LOGICAL)
+
+    greet("cells", peers["cells"][:8])
     loads = [
         pltpu.make_async_copy(a, b, load_sem.at[n]) for n, (a, b) in enumerate(zip(given, held))
     ]
     for n in (3, 2, 4, 5, 1, 7, 0, 6):
         loads[n].start()
-    greet("cells", CELLS_ORDER[8:])
-    greet("dp", DP_ORDER)
+    greet("cells", peers["cells"][8:])
+    greet("dp", peers["dp"])
 
     def send_all(axis, phase, src_of, arrived):
         mine = me_cells if axis == "cells" else me_dp
-        for pattern in ORDERS[axis]:
-            other = peer(axis, pattern)
+        for other, device in peers[axis]:
             pltpu.make_async_remote_copy(
                 src_ref=src_of(other),
                 dst_ref=arrived.at[mine],
                 send_sem=send_sem.at[phase],
                 recv_sem=recv_sem.at[phase],
-                device_id={axis: other},
-                device_id_type=MESH,
+                device_id=device,
+                device_id_type=LOGICAL,
             ).start()
 
     def fold(x):

time: 39.4 us -> 39.4 us (level)
  no operation moved by 1% of the time
where the time goes in v8:
time: 39.4 us; the launch traced here: 39.3 us
  Pallas kernels  38.7 us (98%)
  local copies, waits for them, and re-layouts  0.61 us (2%)
    pallas_call x1, Pallas kernels, on_device(): pl.pallas_call(functools.partial(body, cells * GROUP), out_shape=pltpu.VM...  38.7 us

profile of v8, /device:TPU:1, one launch (start us, length us, event | category | flops | bytes accessed | tf_op | source)
XLA Modules:
  0.0 39.3 jit_solution(14034520639621685106)
XLA Ops:
  0.0 38.7 %shard_map.82 = f32[8,768]{1,0:T(8,128)S(1)} custom-call(bf16[384,768]{1,0:T(8,128)(2,1)} %bitcast.6, bf16[256,768]{1,0:T(8,128)(2,1)} %bitcast.7, s32[1,512]{1,0:T(1,128)} %bitcast.9, s32[1,512]{1,0:T(1,128)} %bitcast.10, f32[1,512]{1,0:T(1,128)} %bitcast.11, s32[8,512]{1,0:T(8,128)} %refs_5_.1, s32[8]{0:T(128)} %refs_6_.1, f32[6,128]{1,0:T(8,128)} %bitcast.8), custom_call_target="tpu_custom_call" | custom-call | tf_op jit(solution)/shard_map/pallas_call | solution.py:324
  38.7 0.6 %copy.10 = f32[8,768]{1,0:T(8,128)} copy(f32[8,768]{1,0:T(8,128)S(1)} %shard_map.82) | data formatting | bytes 49152

commit v9 on v8

--- a/solution.py
+++ b/solution.py
@@ -53,7 +53,7 @@
     cells_total,
     *refs,
 ):
-    given, out_ref, held, refs = refs[:8], refs[8], refs[9:17], refs[17:]
+    given, (base_ref, step_ref), held, refs = refs[:8], refs[8:10], refs[10:18], refs[18:]
     src_ref, rec_ref, sidx_ref, ridx_ref, obs_ref, noise_ref, huber_ref, start_ref = held
     sf, rk, ka, kd, oh, data_s, data_r, tab_s, tab_r, g1_s, g1_r, dl_s, dl_r, q1_s, q1_r = refs[:15]
     g2_s, g2_r, q2_s, q2_r, send_sem, recv_sem, load_sem = refs[15:]
@@ -296,9 +296,9 @@
     second = reduce_gradient(5, whole, g2_s, g2_r, lambda: None)
     send_squares(6, second, q2_s, q2_r)
     velocity = first * inverse1
-    base = (start - 0.1 * velocity) - 0.1 * (0.9 * velocity)
+    base_ref[...] = (start - 0.1 * velocity) - 0.1 * (0.9 * velocity)
     wait_all(recv_sem, 6, q2_r)
-    out_ref[...] = base - 0.1 * (second * inverse_scale(q2_r))
+    step_ref[...] = 0.1 * (second * inverse_scale(q2_r))
 
     for phase, ref in enumerate((data_r, tab_r, g1_r, dl_r, q1_r, g2_r, q2_r)):
         wait_all(send_sem, phase, ref)
@@ -321,11 +321,11 @@
     def pair(shape, dtype):
         return [pltpu.VMEM(shape, dtype), pltpu.VMEM((GROUP,) + shape, dtype)]
 
-    return pl.pallas_call(
+    base, step = pl.pallas_call(
         functools.partial(body, cells * GROUP),
-        out_shape=pltpu.VMEM((REAL, cells), F32),
+        out_shape=[pltpu.VMEM((REAL, cells), F32)] * 2,
         in_specs=[pl.BlockSpec(memory_space=pltpu.HBM)] * 8,
-        out_specs=pl.BlockSpec(memory_space=pltpu.VMEM),
+        out_specs=[pl.BlockSpec(memory_space=pltpu.VMEM)] * 2,
         scratch_shapes=held
         + [
             pltpu.VMEM((COMP, SOURCES, cells), F32),
@@ -358,6 +358,7 @@
         huber,
         start.reshape(-1, 128),
     )
+    return base - step
 
 
 def solution(mesh):

time: 39.4 us -> 39.4 us (level)
  other arithmetic: 0 us -> 0.61 us
  local copies, waits for them, and re-layouts: 0.61 us -> 0 us
    sub x0 -> x1, other arithmetic: none -> 0.61 us  [on_device(): return base - step]
    unnamed x1 -> x0, local copies, waits for them, and re-layouts: 0.61 us -> none
where the time goes in v9:
time: 39.4 us; the launch traced here: 39.3 us
  Pallas kernels  38.7 us (98%)
  other arithmetic  0.61 us (2%)
    pallas_call x1, Pallas kernels, on_device(): pl.pallas_call(functools.partial(body, cells * GROUP), out_shape=[pltpu.V...  38.7 us

profile of v9, /device:TPU:1, one launch (start us, length us, event | category | flops | bytes accessed | tf_op | source)
XLA Modules:
  0.0 39.3 jit_solution(10964696117944701582)
XLA Ops:
  0.0 38.7 %shard_map.82 = (f32[8,768]{1,0:T(8,128)S(1)}, f32[8,768]{1,0:T(8,128)S(1)}) custom-call(bf16[384,768]{1,0:T(8,128)(2,1)} %bitcast.6, bf16[256,768]{1,0:T(8,128)(2,1)} %bitcast.7, s32[1,512]{1,0:T(1,128)} %bitcast.9, s32[1,512]{1,0:T(1,128)} %bitcast.10, f32[1,512]{1,0:T(1,128)} %bitcast.11, s32[8,512]{1,0:T(8,128)} %refs_5_.1, s32[8]{0:T(128)} %refs_6_.1, ...), custom_call_target="tpu_custom_call" | custom-call | tf_op jit(solution)/shard_map/pallas_call | solution.py:324
  38.7 0.6 %sub.3 = f32[8,768]{1,0:T(8,128)} subtract(f32[8,768]{1,0:T(8,128)S(1)} %get-tuple-element.7, f32[8,768]{1,0:T(8,128)S(1)} %get-tuple-element.8) | non-fusion elementwise | flops 6144 | bytes 73728 | tf_op jit(solution)/shard_map/sub | solution.py:361
